TPU v7x, 128 devices: a whole 4x4x4 slice. The times are simulated.
128 devices in a mesh: row: 8 (over y, core), col: 16 (over z, x).
Axes of the slice: x: 4, y: 4, z: 4, core: 2. Of those that a mesh axis runs over, the one named last changes fastest.
Arguments:
- features: bfloat16 [16, 2097152], P(None, ('row', 'col')), may hold values from -6 to 6
- point_weights: bfloat16 [8, 2097152], P(None, ('row', 'col')), may hold values from 0.049804688 to 1
- point_corner: int32 [2097152], P(('row', 'col')), may hold values from 0 to 342
- block_owner: int32 [16384, 1], P(('row', 'col')), may hold values from 0 to 127; in each aligned block of 128 rows (0 to 127, 128 to 255, ...) at most 2 rows name the same one
- block_cell: int32 [16384], P(('row', 'col')), may hold values from 0 to 255
- spec_weight: bfloat16 [64, 64, 16, 16, 128], P('col', 'row'), may hold values from -12 to 12
- skip_weight: bfloat16 [16, 16], replicated, may hold values from -1.5 to 1.5
- mlp_in: bfloat16 [64, 16], replicated, may hold values from -1.5 to 1.5
- mlp_bias: float32 [64], replicated, may hold values from -4 to 4
- mlp_out: bfloat16 [16, 64], replicated, may hold values from -0.75 to 0.75
Outputs:
- point_values: bfloat16 [16, 2097152], P(None, ('row', 'col'))
Inputs may be any that keep to these rules, and one draw needn't show every extreme that they name: `block_owner`: in each aligned block of 128 rows (the point blocks of one device) no device number appears more than 2 times; devices are numbered r * 16 + s over row r and column s.
All inputs are finite; a program needn't handle non-finite values.
Results may differ from a plain program's by a relative error of at most 0.013.
Values may be sent and summed in bfloat16 or wider, within the bound.
No kernel may reach another device: no remote copies, remote signals or barrier semaphores. Data moves between devices by JAX's collectives and lax.ppermute only.
A program may use at most 128 MiB of HBM per device.

v0:
```python
import math
from functools import partial

import jax
import jax.numpy as jnp
import numpy as np
from jax import lax
from jax.experimental import pallas as pl
from jax.experimental.pallas import tpu as pltpu
from jax.sharding import PartitionSpec as P

GRID = 256
MODES = 64
BE = 8
NPTS = 128
NBLK = 128
NSLOT = 256
ROWS = 8
COLS = 16
CH = 16
HID = 64
F32 = jnp.float32
BF16 = jnp.bfloat16
NN = (((1,), (0,)), ((), ()))
NT = (((1,), (1,)), ((), ()))
TN = (((0,), (0,)), ((), ()))


def mm(a, b, dims=NN):
    return lax.dot_general(a, b, dims, preferred_element_type=F32)


def _freqs():
    j = np.arange(MODES)
    return np.where(j < MODES // 2, j, GRID - MODES + j)


def _trig(freq):
    turns = (np.arange(GRID)[:, None] * freq[None, :]) % GRID
    theta = (2.0 * math.pi / GRID) * turns
    f = 1.0 / math.sqrt(GRID)
    return np.cos(theta) * f, np.sin(theta) * f


def tables():
    cz, sz = _trig(np.arange(MODES))
    cf, sf = _trig(_freqs())
    tz = np.stack([cz, -sz], -1).reshape(GRID, 2 * MODES).T
    fwd = np.stack([np.stack([cf, -sf], -1), np.stack([sf, cf], -1)], 1)
    inv = np.stack(
        [np.stack([cf.T, sf.T], -1), np.stack([-sf.T, cf.T], -1)], 1
    )
    ty = fwd.reshape(COLS, 16, 2, ROWS, 8, 2).transpose(3, 5, 4, 0, 2, 1).reshape(128, 512)
    tx = fwd.reshape(ROWS, 4, 8, 2, MODES, 2).transpose(5, 4, 0, 1, 3, 2).reshape(128, 512)
    ix = inv.reshape(MODES, 2, ROWS, 4, 8, 2).transpose(2, 3, 5, 4, 1, 0).reshape(512, 128)
    iy = inv.reshape(ROWS, 8, 2, COLS, 16, 2).transpose(3, 5, 4, 0, 2, 1).reshape(512, 128)
    a = np.where(np.arange(MODES) == 0, 1.0, 2.0)[None, :]
    iz = np.stack([a * cz, -a * sz], -1).reshape(GRID, 2 * MODES)
    return [jnp.asarray(t.astype(np.float32)).astype(BF16) for t in (tz, ty, tx, ix, iy, iz)]


def div_const(v, d):
    return ((v.astype(F32) + 0.5) * (1.0 / d)).astype(jnp.int32)


def pack_kernel(own_ref, cell_ref, feat_ref, w_ref, corner_ref, send_ref, cnt_ref):
    zero = jnp.zeros((8, 32, NPTS), BF16)

    @pl.loop(0, NSLOT // 8)
    def _(i):
        send_ref[pl.ds(i * 8, 8)] = zero

    @pl.loop(0, NBLK)
    def _(i):
        cnt_ref[i] = 0

    row = lax.broadcasted_iota(jnp.int32, (8, NPTS), 0)

    @pl.loop(0, NBLK)
    def _(b):
        o = own_ref[b]
        r = cnt_ref[o]
        cnt_ref[o] = r + 1
        slot = o * 2 + jnp.minimum(r, 1)
        at = pl.multiple_of(b * NPTS, NPTS)
        v = jnp.broadcast_to(corner_ref[pl.ds(b, 1), :], (8, NPTS))
        vx = div_const(v, 49)
        rest = v - vx * 49
        vy = div_const(rest, 7)
        vz = rest - vy * 7
        head = jnp.where(
            row == 0, vx, jnp.where(row == 1, vy, jnp.where(row == 2, vz, cell_ref[b] + 1))
        )
        tail = jnp.concatenate([w_ref[:, pl.ds(at, NPTS)].astype(F32), head.astype(F32)], 0)
        send_ref[slot, 0:16, :] = feat_ref[:, pl.ds(at, NPTS)]
        send_ref[slot, 16:32, :] = tail.astype(BF16)


def pack(owner, cell, features, weights, corner):
    smem = pl.BlockSpec(memory_space=pltpu.SMEM)
    vmem = pl.BlockSpec(memory_space=pltpu.VMEM)
    return pl.pallas_call(
        pack_kernel,
        out_shape=jax.ShapeDtypeStruct((NSLOT, 32, NPTS), BF16),
        in_specs=[smem, smem, vmem, vmem, vmem],
        out_specs=vmem,
        scratch_shapes=[pltpu.SMEM((NBLK,), jnp.int32)],
        name="pack",
    )(owner, cell, features, weights, corner)


def yz_basis(tail):
    zi = lax.broadcasted_iota(jnp.int32, (8, NPTS), 0).astype(F32)
    bc = lambda k: jnp.broadcast_to(tail[k : k + 1, :], (8, NPTS))
    vy, vz = bc(9), bc(10)
    m0 = zi == vz
    m1 = zi == vz + 1.0
    zero = jnp.zeros((8, NPTS), F32)
    zc = [
        [
            jnp.where(m0, bc(4 * dx + 2 * dy), jnp.where(m1, bc(4 * dx + 2 * dy + 1), zero))
            for dy in range(2)
        ]
        for dx in range(2)
    ]
    my = [vy == float(y) for y in range(7)]
    halves = []
    for dx in range(2):
        rows = []
        for y in range(8):
            val = zero
            if y > 0:
                val = jnp.where(my[y - 1], zc[dx][1], val)
            if y < 7:
                val = jnp.where(my[y], zc[dx][0], val)
            rows.append(val)
        halves.append(jnp.concatenate(rows, 0).astype(BF16))
    return jnp.concatenate(halves, 1)


def scatter_kernel(ids_ref, recv_ref, tz_ref, field_ref, out_ref, g_ref, z_ref, *, unroll):
    zero = jnp.zeros((4, 64, 128), F32)

    @pl.loop(0, 64)
    def _(i):
        g_ref[pl.ds(i * 4, 4)] = zero

    @pl.loop(0, NSLOT // unroll)
    def _(i):
        for u in range(unroll):
            s = i * unroll + u
            tail = recv_ref[s, 16:32, :].astype(F32)
            basis = yz_basis(tail)
            feat = recv_ref[s, 0:16, :].astype(F32)
            vx = jnp.broadcast_to(tail[8:9, :], (16, NPTS))
            zf = jnp.zeros((16, NPTS), BF16)
            part = [jnp.where(vx == float(x), feat, 0.0).astype(BF16) for x in range(7)]
            lhs = jnp.concatenate(
                [jnp.concatenate(part + [zf], 0), jnp.concatenate([zf] + part, 0)], 1
            )
            res = mm(basis, lhs, NT)
            b = jnp.maximum(ids_ref[s] - 1, 0)
            g_ref[b] = g_ref[b] + res

    tz = tz_ref[...]

    @pl.loop(0, 8)
    def _(q):
        bx = q // 2
        by = q % 2
        for yl in range(8):
            m = g_ref[pl.ds(q * 32, 32), yl * 8 : yl * 8 + 8, :].reshape(GRID, 128).astype(BF16)
            field_ref[q * 8 + yl] = m
            z_ref[bx, pl.ds(by * 8 + yl, 128, stride=16), :] = mm(tz, m)

    @pl.loop(0, 16)
    def _(s):
        for k in range(8):
            for bx in range(4):
                at = pl.multiple_of(s * 128 + k * 16, 16)
                out_ref[s, k, bx] = z_ref[bx, pl.ds(at, 16), :].astype(BF16)


def scatter(ids, recv, tz):
    smem = pl.BlockSpec(memory_space=pltpu.SMEM)
    vmem = pl.BlockSpec(memory_space=pltpu.VMEM)
    return pl.pallas_call(
        partial(scatter_kernel, unroll=4),
        out_shape=(
            jax.ShapeDtypeStruct((64, GRID, 128), BF16),
            jax.ShapeDtypeStruct((16, 8, 4, 16, 128), BF16),
        ),
        in_specs=[smem, vmem, vmem],
        out_specs=(vmem, vmem),
        scratch_shapes=[pltpu.VMEM((256, 64, 128), F32), pltpu.VMEM((4, 2048, 128), F32)],
        name="scatter_z",
    )(ids, recv, tz)


def y_kernel(in_ref, t_ref, out_ref):
    t = t_ref[...]
    for kz in range(4):
        for h in range(2):
            rhs = jnp.concatenate(
                [in_ref[:, 2 * kz : 2 * kz + 2, 2 * h + e].reshape(512, 128) for e in range(2)], 1
            )
            res = mm(t, rhs).astype(BF16)
            for r in range(8):
                for e in range(2):
                    out_ref[r, kz, 2 * h + e] = res[r * 16 : r * 16 + 16, e * 128 : e * 128 + 128]


def y_forward(zs, ty):
    return pl.pallas_call(
        y_kernel,
        out_shape=jax.ShapeDtypeStruct((8, 4, 4, 16, 128), BF16),
        name="y_forward",
    )(zs, ty)


def block_transpose(x):
    si = lax.broadcasted_iota(jnp.int32, x.shape, 1)
    gi = lax.broadcasted_iota(jnp.int32, x.shape, 2) // 16
    for k in range(3):
        d = 1 << k
        mi = (si // d) % 2
        mg = (gi // d) % 2
        up = pltpu.roll(pltpu.roll(x, 8 - d, 1), 16 * d, 2)
        if k == 2:
            x = jnp.where(mi == mg, x, up)
        else:
            down = pltpu.roll(pltpu.roll(x, d, 1), 128 - 16 * d, 2)
            x = jnp.where(mi == mg, x, jnp.where(mi < mg, up, down))
    return x


def x_kernel(in_ref, w_ref, tx_ref, ix_ref, out_ref):
    data = in_ref[...].astype(F32).reshape(64, 8, 128)
    data = block_transpose(data).reshape(512, 128).astype(BF16)
    spec = mm(tx_ref[...], data).T.astype(BF16).astype(F32)
    swapped = pltpu.roll(spec, 64, 1)
    lane = lax.broadcasted_iota(jnp.int32, (16, 128), 1)
    parts = []
    for ky in range(8):
        a1 = jnp.zeros((16, 128), F32)
        a2 = jnp.zeros((16, 128), F32)
        for c in range(CH):
            w = w_ref[0, ky, c].astype(F32)
            at = ky * 16 + c
            a1 = a1 + spec[at : at + 1, :] * w
            a2 = a2 + swapped[at : at + 1, :] * w
        parts.append(
            jnp.where(lane < 64, a1 - pltpu.roll(a1, 64, 1), a2 + pltpu.roll(a2, 64, 1))
        )
    mixed = jnp.concatenate(parts, 0).astype(BF16)
    xi = mm(ix_ref[...], mixed, NT)
    xi = block_transpose(xi.reshape(64, 8, 128))
    out_ref[...] = xi.reshape(8, 1, 4, 16, 128).astype(BF16)


def x_mix(ys, weight, tx, ix):
    whole = lambda k: (0, 0)
    return pl.pallas_call(
        x_kernel,
        grid=(4,),
        out_shape=jax.ShapeDtypeStruct((8, 4, 4, 16, 128), BF16),
        in_specs=[
            pl.BlockSpec((8, 1, 4, 16, 128), lambda k: (0, k, 0, 0, 0)),
            pl.BlockSpec((1, 8, 16, 16, 128), lambda k: (k, 0, 0, 0, 0)),
            pl.BlockSpec((128, 512), whole),
            pl.BlockSpec((512, 128), whole),
        ],
        out_specs=pl.BlockSpec((8, 1, 4, 16, 128), lambda k: (0, k, 0, 0, 0)),
        name="x_mix",
    )(ys, weight, tx, ix)


def yi_kernel(in_ref, t_ref, out_ref):
    t = t_ref[...]
    for kz in range(4):
        for h in range(2):
            rhs = jnp.concatenate(
                [in_ref[:, kz, 2 * h + e].reshape(128, 128) for e in range(2)], 1
            )
            res = mm(t, rhs).astype(BF16)
            for s in range(16):
                for ri in range(2):
                    at = s * 32 + ri * 16
                    for e in range(2):
                        out_ref[s, 2 * kz + ri, 2 * h + e] = res[
                            at : at + 16, e * 128 : e * 128 + 128
                        ]


def y_inverse(xs, iy):
    return pl.pallas_call(
        yi_kernel,
        out_shape=jax.ShapeDtypeStruct((16, 8, 4, 16, 128), BF16),
        name="y_inverse",
    )(xs, iy)


def final_kernel(
    ids_ref, yi_ref, field_ref, tail_ref, iz_ref, sk_ref, w1_ref, b1_ref, w2_ref,
    out_ref, y_ref, l_ref, *, unroll
):
    @pl.loop(0, 16)
    def _(s):
        for k in range(8):
            for bx in range(4):
                at = pl.multiple_of(s * 128 + k * 16, 16)
                y_ref[bx, pl.ds(at, 16), :] = yi_ref[s, k, bx].astype(F32)

    iz = iz_ref[...]
    sk = sk_ref[...]
    w1 = w1_ref[...]
    w2 = w2_ref[...]
    b1 = b1_ref[...]

    @pl.loop(0, 64)
    def _(i):
        bx = i // 16
        y = i % 16
        rhs = y_ref[bx, pl.ds(y, 128, stride=16), :].astype(BF16)
        pre = (mm(iz, rhs) + mm(field_ref[i], sk)).astype(BF16)
        h = jax.nn.gelu(mm(pre, w1) + b1).astype(BF16)
        l_ref[i] = mm(h, w2).astype(BF16).astype(F32)

    @pl.loop(0, NSLOT // unroll)
    def _(i):
        for u in range(unroll):
            s = i * unroll + u
            tail = tail_ref[s].astype(F32)
            basis = yz_basis(tail)
            b = jnp.maximum(ids_ref[s] - 1, 0)
            q = b // 32
            at = pl.multiple_of((b % 32) * 8, 8)
            cells = l_ref[pl.ds(q * 8, 8), pl.ds(at, 8), :].reshape(64, 128).astype(BF16)
            res = mm(cells, basis, TN)
            vx = jnp.broadcast_to(tail[8:9, :], (16, NPTS))
            val = jnp.zeros((16, NPTS), F32)
            for x in range(7):
                got = res[x * 16 : x * 16 + 16, 0:128] + res[x * 16 + 16 : x * 16 + 32, 128:256]
                val = jnp.where(vx == float(x), got, val)
            out_ref[s] = val.astype(BF16)


def final(ids, yi, field, recv, iz, sk, w1, b1, w2):
    smem = pl.BlockSpec(memory_space=pltpu.SMEM)
    vmem = pl.BlockSpec(memory_space=pltpu.VMEM)
    return pl.pallas_call(
        partial(final_kernel, unroll=4),
        grid=(1,),
        out_shape=jax.ShapeDtypeStruct((NSLOT, 16, NPTS), BF16),
        in_specs=[
            smem,
            vmem,
            vmem,
            pl.BlockSpec((NSLOT, 16, NPTS), lambda i: (0, 1, 0)),
            vmem,
            vmem,
            vmem,
            vmem,
            vmem,
        ],
        out_specs=vmem,
        scratch_shapes=[pltpu.VMEM((4, 2048, 128), F32), pltpu.VMEM((64, GRID, 128), F32)],
        name="mlp_gather",
    )(ids, yi, field, recv, iz, sk, w1, b1, w2)


def unpack_kernel(own_ref, in_ref, out_ref, cnt_ref):
    @pl.loop(0, NBLK)
    def _(i):
        cnt_ref[i] = 0

    @pl.loop(0, NBLK)
    def _(b):
        o = own_ref[b]
        r = cnt_ref[o]
        cnt_ref[o] = r + 1
        slot = o * 2 + jnp.minimum(r, 1)
        at = pl.multiple_of(b * NPTS, NPTS)
        out_ref[:, pl.ds(at, NPTS)] = in_ref[slot]


def unpack(owner, vals):
    smem = pl.BlockSpec(memory_space=pltpu.SMEM)
    vmem = pl.BlockSpec(memory_space=pltpu.VMEM)
    return pl.pallas_call(
        unpack_kernel,
        out_shape=jax.ShapeDtypeStruct((CH, NBLK * NPTS), BF16),
        in_specs=[smem, vmem],
        out_specs=vmem,
        scratch_shapes=[pltpu.SMEM((NBLK,), jnp.int32)],
        name="unpack",
    )(owner, vals)


def a2a(x, axes):
    return lax.all_to_all(x, axes, split_axis=0, concat_axis=0, tiled=True)


def body(
    features,
    point_weights,
    point_corner,
    block_owner,
    block_cell,
    spec_weight,
    skip_weight,
    mlp_in,
    mlp_bias,
    mlp_out,
):
    tz, ty, tx, ix, iy, iz = tables()
    eye = jnp.eye(8, dtype=BF16)
    sk = jnp.kron(eye, skip_weight.T)
    w1 = jnp.kron(eye, mlp_in.T)
    w2 = jnp.kron(eye, mlp_out.T)
    b1 = jnp.tile(mlp_bias, 8)[None, :]
    owner = block_owner.reshape(NBLK)
    send = pack(owner, block_cell, features, point_weights, point_corner.reshape(NBLK, NPTS))
    recv = a2a(send, ("row", "col"))
    ids = recv[:, 27, 0].astype(jnp.int32)
    field, zs = scatter(ids, recv, tz)
    zs = a2a(zs, "col")
    ys = y_forward(zs, ty)
    ys = a2a(ys, "row")
    xs = x_mix(ys, spec_weight, tx, ix)
    xs = a2a(xs, "row")
    yi = y_inverse(xs, iy)
    yi = a2a(yi, "col")
    vals = final(ids, yi, field, recv, iz, sk, w1, b1, w2)
    vals = a2a(vals, ("row", "col"))
    return unpack(owner, vals)


def solution(mesh):
    return jax.shard_map(
        body,
        mesh=mesh,
        in_specs=(
            P(None, ("row", "col")),
            P(None, ("row", "col")),
            P(("row", "col")),
            P(("row", "col"), None),
            P(("row", "col")),
            P("col", "row", None, None, None),
            P(),
            P(),
            P(),
            P(),
        ),
        out_specs=P(None, ("row", "col")),
        check_vma=False,
    )
```

profile of v0, /device:TPU:1, one launch (start us, length us, event | category | flops | bytes accessed | tf_op | source)
XLA Modules:
  0.0 276.4 jit_solution(7085103617390787115)
XLA Ops:
  0.0 6.2 %pack.1 = bf16[256,32,128]{2,1,0:T(8,128)(2,1)} custom-call(s32[128]{0:T(128)} %bitcast.17, s32[128]{0:T(128)} %cell_ref.1, bf16[16,16384]{1,0:T(8,128)(2,1)} %feat_ref.1, bf16[8,16384]{1,0:T(8,128)(2,1)} %w_ref.2, s32[128,128]{1,0:T(8,128)} %bitcast.13), custom_call_target="tpu_custom_call" | custom-call | tf_op jit(solution)/shard_map/pack/pallas_call | solution.py:102
  6.2 40.9 %all_to_all.30.recv_ref.tail_ref = bf16[256,32,128]{2,1,0:T(8,128)(2,1)S(1)} all-to-all(bf16[256,32,128]{2,1,0:T(8,128)(2,1)} %pack.1), channel_id=1, replica_groups=mesh['row'=8,'col'=16] {'row','col'}, dimensions={0} | all-to-all | bytes 4194304 | tf_op jit(solution)/shard_map/all_to_all | solution.py:401
  47.1 5.2 %fusion.ids_ref = s32[256]{0:T(256)} fusion(bf16[256,32,128]{2,1,0:T(8,128)(2,1)S(1)} %all_to_all.30.recv_ref.tail_ref), kind=kLoop, calls=%fused_computation.1 | loop fusion | flops 256 | bytes 1536 | tf_op jit(solution)/shard_map/convert_element_type | solution.py:425
  52.3 22.0 %scatter_z.1 = (bf16[64,256,128]{2,1,0:T(8,128)(2,1)}, bf16[16,8,4,16,128]{4,3,2,1,0:T(8,128)(2,1)}) custom-call(s32[256]{0:T(256)} %fusion.ids_ref, bf16[256,32,128]{2,1,0:T(8,128)(2,1)} %copy-done, bf16[128,256]{1,0:T(8,128)(2,1)} %constant.19.tz_ref), custom_call_target="tpu_custom_call" | custom-call | tf_op jit(solution)/shard_map/scatter_z/pallas_call | solution.py:187
  74.3 31.5 %all_to_all.31.in_ref = bf16[16,8,4,16,128]{4,3,2,1,0:T(8,128)(2,1)} all-to-all(bf16[16,8,4,16,128]{4,3,2,1,0:T(8,128)(2,1)} %get-tuple-element.7), channel_id=1, replica_groups=mesh['row'=8,'col'=16] {'col'}, dimensions={0} | all-to-all | bytes 4194304 | tf_op jit(solution)/shard_map/all_to_all | solution.py:401
  105.8 2.8 %y_forward.1 = bf16[8,4,4,16,128]{4,3,2,1,0:T(8,128)(2,1)} custom-call(bf16[16,8,4,16,128]{4,3,2,1,0:T(8,128)(2,1)} %all_to_all.31.in_ref, bf16[128,512]{1,0:T(8,128)(2,1)} %constant.20.t_ref), custom_call_target="tpu_custom_call" | custom-call | tf_op jit(solution)/shard_map/y_forward/pallas_call | solution.py:214
  108.6 15.7 %all_to_all.32.in_ref = bf16[8,4,4,16,128]{4,3,2,1,0:T(8,128)(2,1)} all-to-all(bf16[8,4,4,16,128]{4,3,2,1,0:T(8,128)(2,1)} %y_forward.1), channel_id=1, replica_groups=mesh['row'=8,'col'=16] {'row'}, dimensions={0} | all-to-all | bytes 1048576 | tf_op jit(solution)/shard_map/all_to_all | solution.py:401
  124.3 7.0 %x_mix.1 = bf16[8,4,4,16,128]{4,3,2,1,0:T(8,128)(2,1)} custom-call(bf16[8,4,4,16,128]{4,3,2,1,0:T(8,128)(2,1)} %all_to_all.32.in_ref, bf16[4,8,16,16,128]{4,3,2,1,0:T(8,128)(2,1)} %w_ref.3, bf16[128,512]{1,0:T(8,128)(2,1)} %constant.21.tx_ref, bf16[512,128]{1,0:T(8,128)(2,1)} %constant.22.ix_ref), custom_call_target="tpu_custom_call" | custom-call | tf_op jit(solution)/shard_map/x_mix/pallas_call | solution.py:263
  131.3 14.5 %all_to_all.33.in_ref = bf16[8,4,4,16,128]{4,3,2,1,0:T(8,128)(2,1)} all-to-all(bf16[8,4,4,16,128]{4,3,2,1,0:T(8,128)(2,1)} %x_mix.1), channel_id=1, replica_groups=mesh['row'=8,'col'=16] {'row'}, dimensions={0} | all-to-all | bytes 1048576 | tf_op jit(solution)/shard_map/all_to_all | solution.py:401
  145.8 3.1 %y_inverse.1 = bf16[16,8,4,16,128]{4,3,2,1,0:T(8,128)(2,1)} custom-call(bf16[8,4,4,16,128]{4,3,2,1,0:T(8,128)(2,1)} %all_to_all.33.in_ref, bf16[512,128]{1,0:T(8,128)(2,1)} %constant.23.t_ref), custom_call_target="tpu_custom_call" | custom-call | tf_op jit(solution)/shard_map/y_inverse/pallas_call | solution.py:296
  148.9 3.8 %all-to-all-start.4 = ((bf16[16,8,4,16,128]{4,3,2,1,0:T(8,128)(2,1)}), bf16[16,8,4,16,128]{4,3,2,1,0:T(8,128)(2,1)S(1)}, u32[]{:S(2)}, u32[]{:S(2)}) async-start(bf16[16,8,4,16,128]{4,3,2,1,0:T(8,128)(2,1)} %y_inverse.1), calls=%async_computation.4 | async-start | bytes 4194304 | tf_op jit(solution)/shard_map/all_to_all | solution.py:401
  152.9 0.1 broadcast_multiply_fusion.1
  153.0 0.9 mul.79.w1_ref
  153.9 0.1 broadcast_multiply_fusion.2
  154.0 0.8 mul.75.sk_ref
  154.8 0.1 broadcast_multiply_fusion
  154.9 0.2 mul.83
  155.1 0.8 copy.22.w2_ref
  155.9 0.7 broadcast_in_dim_tile.3.b1_ref
  156.6 26.6 %all-to-all-done.4.yi_ref = bf16[16,8,4,16,128]{4,3,2,1,0:T(8,128)(2,1)S(1)} async-done(((bf16[16,8,4,16,128]{4,3,2,1,0:T(8,128)(2,1)}), bf16[16,8,4,16,128]{4,3,2,1,0:T(8,128)(2,1)S(1)}, u32[]{:S(2)}, u32[]{:S(2)}) %all-to-all-start.4) | async-done | bytes 2097184 | tf_op jit(solution)/shard_map/all_to_all | solution.py:401
  183.2 1.3 copy-done.1
  184.5 61.6 %mlp_gather.1 = bf16[256,16,128]{2,1,0:T(8,128)(2,1)} custom-call(s32[256]{0:T(256)} %fusion.ids_ref, bf16[16,8,4,16,128]{4,3,2,1,0:T(8,128)(2,1)} %copy-done.1, bf16[64,256,128]{2,1,0:T(8,128)(2,1)} %get-tuple-element.8.field_ref, bf16[256,32,128]{2,1,0:T(8,128)(2,1)} %copy-done, bf16[256,128]{1,0:T(8,128)(2,1)} %constant.24.iz_ref, ...), custom_call_target="tpu_custom_call" | custom-call | tf_op jit(solution)/shard_map/mlp_gather/pallas_call | solution.py:351
  246.1 26.0 %all_to_all.34.in_ref = bf16[256,16,128]{2,1,0:T(8,128)(2,1)} all-to-all(bf16[256,16,128]{2,1,0:T(8,128)(2,1)} %mlp_gather.1), channel_id=1, replica_groups=mesh['row'=8,'col'=16] {'row','col'}, dimensions={0} | all-to-all | bytes 2097152 | tf_op jit(solution)/shard_map/all_to_all | solution.py:401
  272.1 4.2 %unpack.1 = bf16[16,16384]{1,0:T(8,128)(2,1)} custom-call(s32[128]{0:T(128)} %bitcast.18, bf16[256,16,128]{2,1,0:T(8,128)(2,1)} %all_to_all.34.in_ref), custom_call_target="tpu_custom_call" | custom-call | tf_op jit(solution)/shard_map/unpack/pallas_call | solution.py:390
  (15 shorter events, 0.2 us)
Async XLA Ops:
  47.1 5.2 %copy-start = (bf16[256,32,128]{2,1,0:T(8,128)(2,1)}, bf16[256,32,128]{2,1,0:T(8,128)(2,1)S(1)}, u32[]{:S(2)}) copy-start(bf16[256,32,128]{2,1,0:T(8,128)(2,1)S(1)} %all_to_all.30.recv_ref.tail_ref) | copy-start | bytes 6291460
  148.9 4.0 %copy-start.2 = (bf16[64,16]{0,1:T(8,128)(2,1)S(1)}, bf16[64,16]{0,1:T(8,128)(2,1)}, u32[]{:S(2)}) copy-start(bf16[64,16]{0,1:T(8,128)(2,1)} %param.23) | copy-start | bytes 6148
  148.9 4.9 %copy-start.4 = (bf16[16,16]{1,0:T(8,128)(2,1)S(1)}, bf16[16,16]{1,0:T(8,128)(2,1)}, u32[]{:S(2)}) copy-start(bf16[16,16]{1,0:T(8,128)(2,1)} %param.22) | copy-start | bytes 1540
  148.9 5.9 %copy-start.3 = (bf16[16,64]{1,0:T(8,128)(2,1)S(1)}, bf16[16,64]{1,0:T(8,128)(2,1)}, u32[]{:S(2)}) copy-start(bf16[16,64]{1,0:T(8,128)(2,1)} %param.25) | copy-start | bytes 6148
  148.9 34.3 %all-to-all-start.4 = ((bf16[16,8,4,16,128]{4,3,2,1,0:T(8,128)(2,1)}), bf16[16,8,4,16,128]{4,3,2,1,0:T(8,128)(2,1)S(1)}, u32[]{:S(2)}, u32[]{:S(2)}) async-start(bf16[16,8,4,16,128]{4,3,2,1,0:T(8,128)(2,1)} %y_inverse.1), calls=%async_computation.4 | async-start | bytes 4194304 | tf_op jit(solution)/shard_map/all_to_all | solution.py:401
  152.8 3.1 %copy-start.5 = (f32[64]{0:T(128)S(1)}, f32[64]{0:T(128)}, u32[]{:S(2)}) copy-start(f32[64]{0:T(128)} %param.24) | copy-start | bytes 772
  183.2 1.3 copy-start.1
where the time goes:
time: 277 us; the launch traced here: 276 us
  blocking collectives  129 us (47%)
  Pallas kernels  107 us (39%)
  waiting for transfers between devices  26.6 us (10%)
  other arithmetic  5.44 us (2%)
  local copies, waits for them, and re-layouts  4.84 us (2%)
  starting transfers between devices  3.85 us (1%)
    all_to_all x5, blocking collectives, a2a(): return lax.all_to_all(x, axes, split_axis=0, concat_axis=0, tiled=True)  129 us
    pallas_call x1, Pallas kernels, final(): pl.pallas_call(partial(final_kernel, unroll=4), grid=(1,), out_shape=jax....  61.6 us
    all_to_all x1, waiting for transfers between devices, a2a(): return lax.all_to_all(x, axes, split_axis=0, concat_axis=0, tiled=True)  26.6 us
    pallas_call x1, Pallas kernels, scatter(): pl.pallas_call(partial(scatter_kernel, unroll=4), out_shape=(jax.ShapeDty...  22 us
    pallas_call x1, Pallas kernels, x_mix(): pl.pallas_call(x_kernel, grid=(4,), out_shape=jax.ShapeDtypeStruct((8, 4,...  7.01 us
    pallas_call x1, Pallas kernels, pack(): pl.pallas_call(pack_kernel, out_shape=jax.ShapeDtypeStruct((NSLOT, 32, NP...  6.17 us
  transfers between devices with their start and end apart: 1, of which 1 were waited for; matrix products, arithmetic and copies ran while one was open for 1% of the time, Pallas kernels for 0%

commit v1 on v0

--- a/solution.py
+++ b/solution.py
@@ -70,13 +70,13 @@
     def _(i):
         send_ref[pl.ds(i * 8, 8)] = zero
 
-    @pl.loop(0, NBLK)
+    @pl.loop(0, NBLK, unroll=16)
     def _(i):
         cnt_ref[i] = 0
 
     row = lax.broadcasted_iota(jnp.int32, (8, NPTS), 0)
 
-    @pl.loop(0, NBLK)
+    @pl.loop(0, NBLK, unroll=8)
     def _(b):
         o = own_ref[b]
         r = cnt_ref[o]
@@ -138,40 +138,71 @@
     return jnp.concatenate(halves, 1)
 
 
-def scatter_kernel(ids_ref, recv_ref, tz_ref, field_ref, out_ref, g_ref, z_ref, *, unroll):
+def scatter_kernel(
+    recv_hbm, tz_ref, field_hbm, out_hbm, ids_ref,
+    recv_ref, g_ref, z_ref, field_ref, out_ref, in_sem, field_sem, out_sem, *, unroll
+):
+    part = NSLOT // 4
+
+    def fetch(k):
+        at = pl.ds(k * part, part)
+        return pltpu.make_async_copy(recv_hbm.at[at], recv_ref.at[at], in_sem.at[k])
+
+    for k in range(4):
+        fetch(k).start()
     zero = jnp.zeros((4, 64, 128), F32)
 
     @pl.loop(0, 64)
     def _(i):
         g_ref[pl.ds(i * 4, 4)] = zero
 
-    @pl.loop(0, NSLOT // unroll)
-    def _(i):
-        for u in range(unroll):
-            s = i * unroll + u
-            tail = recv_ref[s, 16:32, :].astype(F32)
-            basis = yz_basis(tail)
-            feat = recv_ref[s, 0:16, :].astype(F32)
-            vx = jnp.broadcast_to(tail[8:9, :], (16, NPTS))
-            zf = jnp.zeros((16, NPTS), BF16)
-            part = [jnp.where(vx == float(x), feat, 0.0).astype(BF16) for x in range(7)]
-            lhs = jnp.concatenate(
-                [jnp.concatenate(part + [zf], 0), jnp.concatenate([zf] + part, 0)], 1
-            )
-            res = mm(basis, lhs, NT)
-            b = jnp.maximum(ids_ref[s] - 1, 0)
-            g_ref[b] = g_ref[b] + res
+    @pl.loop(0, 4)
+    def _(k):
+        fetch(k).wait()
+
+        @pl.loop(0, part // unroll)
+        def _(i):
+            for u in range(unroll):
+                s = k * part + i * unroll + u
+                tail = recv_ref[s, 16:32, :].astype(F32)
+                basis = yz_basis(tail)
+                feat = recv_ref[s, 0:16, :].astype(F32)
+                vx = jnp.broadcast_to(tail[8:9, :], (16, NPTS))
+                zf = jnp.zeros((16, NPTS), BF16)
+                sel = [jnp.where(vx == float(x), feat, 0.0).astype(BF16) for x in range(7)]
+                lhs = jnp.concatenate(
+                    [jnp.concatenate(sel + [zf], 0), jnp.concatenate([zf] + sel, 0)], 1
+                )
+                res = mm(basis, lhs, NT)
+                b = jnp.clip(tail[11, 0].astype(jnp.int32) - 1, 0, 255)
+                ids_ref[s] = b
+                g_ref[b] = g_ref[b] + res
 
     tz = tz_ref[...]
+
+    def put_field(q):
+        at = pl.ds(q * 8, 8)
+        return pltpu.make_async_copy(field_ref.at[at], field_hbm.at[at], field_sem.at[q])
+
+    def put_out(s):
+        return pltpu.make_async_copy(out_ref.at[s], out_hbm.at[s], out_sem.at[s])
 
     @pl.loop(0, 8)
     def _(q):
         bx = q // 2
         by = q % 2
-        for yl in range(8):
-            m = g_ref[pl.ds(q * 32, 32), yl * 8 : yl * 8 + 8, :].reshape(GRID, 128).astype(BF16)
-            field_ref[q * 8 + yl] = m
-            z_ref[bx, pl.ds(by * 8 + yl, 128, stride=16), :] = mm(tz, m)
+        for h in range(4):
+            ms = []
+            for yl in (2 * h, 2 * h + 1):
+                m = g_ref[pl.ds(q * 32, 32), yl * 8 : yl * 8 + 8, :].reshape(GRID, 128)
+                m = m.astype(BF16)
+                field_ref[q * 8 + yl] = m
+                ms.append(m)
+            res = mm(tz, jnp.concatenate(ms, 1))
+            for e in range(2):
+                y = by * 8 + 2 * h + e
+                z_ref[bx, pl.ds(y, 128, stride=16), :] = res[:, e * 128 : e * 128 + 128]
+        put_field(q).start()
 
     @pl.loop(0, 16)
     def _(s):
@@ -179,22 +210,42 @@
             for bx in range(4):
                 at = pl.multiple_of(s * 128 + k * 16, 16)
                 out_ref[s, k, bx] = z_ref[bx, pl.ds(at, 16), :].astype(BF16)
-
-
-def scatter(ids, recv, tz):
+        put_out(s).start()
+
+    @pl.loop(0, 8)
+    def _(q):
+        put_field(q).wait()
+
+    @pl.loop(0, 16)
+    def _(s):
+        put_out(s).wait()
+
+
+def scatter(recv, tz):
     smem = pl.BlockSpec(memory_space=pltpu.SMEM)
     vmem = pl.BlockSpec(memory_space=pltpu.VMEM)
-    return pl.pallas_call(
-        partial(scatter_kernel, unroll=4),
+    hbm = pl.BlockSpec(memory_space=pl.ANY)
+    return pl.pallas_call(
+        partial(scatter_kernel, unroll=16),
         out_shape=(
             jax.ShapeDtypeStruct((64, GRID, 128), BF16),
             jax.ShapeDtypeStruct((16, 8, 4, 16, 128), BF16),
+            jax.ShapeDtypeStruct((NSLOT,), jnp.int32),
         ),
-        in_specs=[smem, vmem, vmem],
-        out_specs=(vmem, vmem),
-        scratch_shapes=[pltpu.VMEM((256, 64, 128), F32), pltpu.VMEM((4, 2048, 128), F32)],
+        in_specs=[hbm, vmem],
+        out_specs=(hbm, hbm, smem),
+        scratch_shapes=[
+            pltpu.VMEM((NSLOT, 32, NPTS), BF16),
+            pltpu.VMEM((256, 64, 128), F32),
+            pltpu.VMEM((4, 2048, 128), F32),
+            pltpu.VMEM((64, GRID, 128), BF16),
+            pltpu.VMEM((16, 8, 4, 16, 128), BF16),
+            pltpu.SemaphoreType.DMA((4,)),
+            pltpu.SemaphoreType.DMA((8,)),
+            pltpu.SemaphoreType.DMA((16,)),
+        ],
         name="scatter_z",
-    )(ids, recv, tz)
+    )(recv, tz)
 
 
 def y_kernel(in_ref, t_ref, out_ref):
@@ -300,31 +351,70 @@
     )(xs, iy)
 
 
+def gelu(x):
+    x = x.astype(BF16)
+    c = math.sqrt(2.0 / math.pi)
+    t = jnp.tanh(x * (jnp.asarray(c, BF16) + jnp.asarray(c * 0.044715, BF16) * (x * x)))
+    h = x * jnp.asarray(0.5, BF16)
+    return h + h * t
+
+
 def final_kernel(
-    ids_ref, yi_ref, field_ref, tail_ref, iz_ref, sk_ref, w1_ref, b1_ref, w2_ref,
-    out_ref, y_ref, l_ref, *, unroll
+    ids_ref, yi_hbm, field_hbm, recv_hbm, iz_ref, w1_ref, b1_ref, w2_ref, out_hbm,
+    yi_ref, field_ref, tail_ref, out_ref, y_ref, x_ref, l_ref,
+    yi_sem, field_sem, tail_sem, out_sem, *, ny, unroll
 ):
+    def get_yi(s):
+        return pltpu.make_async_copy(yi_hbm.at[s], yi_ref.at[s], yi_sem.at[s])
+
+    def get_field(i):
+        at = pl.ds(i * ny, ny)
+        return pltpu.make_async_copy(field_hbm.at[at], field_ref.at[at], field_sem.at[i])
+
+    def put_out(i):
+        at = pl.ds(i * unroll, unroll)
+        return pltpu.make_async_copy(out_ref.at[at], out_hbm.at[at], out_sem.at[i])
+
+    get_tail = pltpu.make_async_copy(recv_hbm.at[:, 16:32], tail_ref, tail_sem)
+
     @pl.loop(0, 16)
     def _(s):
+        get_yi(s).start()
+
+    @pl.loop(0, 64 // ny)
+    def _(i):
+        get_field(i).start()
+
+    get_tail.start()
+
+    @pl.loop(0, 16)
+    def _(s):
+        get_yi(s).wait()
         for k in range(8):
             for bx in range(4):
                 at = pl.multiple_of(s * 128 + k * 16, 16)
                 y_ref[bx, pl.ds(at, 16), :] = yi_ref[s, k, bx].astype(F32)
 
-    iz = iz_ref[...]
-    sk = sk_ref[...]
-    w1 = w1_ref[...]
-    w2 = w2_ref[...]
-    b1 = b1_ref[...]
-
-    @pl.loop(0, 64)
-    def _(i):
-        bx = i // 16
-        y = i % 16
-        rhs = y_ref[bx, pl.ds(y, 128, stride=16), :].astype(BF16)
-        pre = (mm(iz, rhs) + mm(field_ref[i], sk)).astype(BF16)
-        h = jax.nn.gelu(mm(pre, w1) + b1).astype(BF16)
-        l_ref[i] = mm(h, w2).astype(BF16).astype(F32)
+    @pl.loop(0, 64 // ny)
+    def _(i):
+        base = i * ny
+        bx = base // 16
+        get_field(i).wait()
+        for p in range(ny // 2):
+            y = (base + 2 * p) % 16
+            rhs = jnp.concatenate(
+                [y_ref[bx, pl.ds(y + e, 128, stride=16), :] for e in range(2)], 1
+            ).astype(BF16)
+            res = mm(iz_ref[...], rhs).astype(BF16)
+            for e in range(2):
+                at = (2 * p + e) * GRID
+                x_ref[at : at + GRID, 0:128] = res[:, e * 128 : e * 128 + 128]
+                x_ref[at : at + GRID, 128:256] = field_ref[base + 2 * p + e]
+        h = gelu(mm(x_ref[...], w1_ref[...]) + b1_ref[...])
+        o = mm(h, w2_ref[...]).astype(BF16).astype(F32)
+        l_ref[pl.ds(base, ny)] = o.reshape(ny, GRID, 128)
+
+    get_tail.wait()
 
     @pl.loop(0, NSLOT // unroll)
     def _(i):
@@ -332,7 +422,7 @@
             s = i * unroll + u
             tail = tail_ref[s].astype(F32)
             basis = yz_basis(tail)
-            b = jnp.maximum(ids_ref[s] - 1, 0)
+            b = ids_ref[s]
             q = b // 32
             at = pl.multiple_of((b % 32) * 8, 8)
             cells = l_ref[pl.ds(q * 8, 8), pl.ds(at, 8), :].reshape(64, 128).astype(BF16)
@@ -343,38 +433,46 @@
                 got = res[x * 16 : x * 16 + 16, 0:128] + res[x * 16 + 16 : x * 16 + 32, 128:256]
                 val = jnp.where(vx == float(x), got, val)
             out_ref[s] = val.astype(BF16)
-
-
-def final(ids, yi, field, recv, iz, sk, w1, b1, w2):
+        put_out(i).start()
+
+    @pl.loop(0, NSLOT // unroll)
+    def _(i):
+        put_out(i).wait()
+
+
+def final(ids, yi, field, recv, iz, w1, b1, w2):
     smem = pl.BlockSpec(memory_space=pltpu.SMEM)
     vmem = pl.BlockSpec(memory_space=pltpu.VMEM)
-    return pl.pallas_call(
-        partial(final_kernel, unroll=4),
-        grid=(1,),
+    hbm = pl.BlockSpec(memory_space=pl.ANY)
+    ny, unroll = 8, 32
+    return pl.pallas_call(
+        partial(final_kernel, ny=ny, unroll=unroll),
         out_shape=jax.ShapeDtypeStruct((NSLOT, 16, NPTS), BF16),
-        in_specs=[
-            smem,
-            vmem,
-            vmem,
-            pl.BlockSpec((NSLOT, 16, NPTS), lambda i: (0, 1, 0)),
-            vmem,
-            vmem,
-            vmem,
-            vmem,
-            vmem,
+        in_specs=[smem, hbm, hbm, hbm, vmem, vmem, vmem, vmem],
+        out_specs=hbm,
+        scratch_shapes=[
+            pltpu.VMEM((16, 8, 4, 16, 128), BF16),
+            pltpu.VMEM((64, GRID, 128), BF16),
+            pltpu.VMEM((NSLOT, 16, NPTS), BF16),
+            pltpu.VMEM((NSLOT, 16, NPTS), BF16),
+            pltpu.VMEM((4, 2048, 128), F32),
+            pltpu.VMEM((ny * GRID, 256), BF16),
+            pltpu.VMEM((64, GRID, 128), F32),
+            pltpu.SemaphoreType.DMA((16,)),
+            pltpu.SemaphoreType.DMA((64 // ny,)),
+            pltpu.SemaphoreType.DMA,
+            pltpu.SemaphoreType.DMA((NSLOT // unroll,)),
         ],
-        out_specs=vmem,
-        scratch_shapes=[pltpu.VMEM((4, 2048, 128), F32), pltpu.VMEM((64, GRID, 128), F32)],
         name="mlp_gather",
-    )(ids, yi, field, recv, iz, sk, w1, b1, w2)
+    )(ids, yi, field, recv, iz, w1, b1, w2)
 
 
 def unpack_kernel(own_ref, in_ref, out_ref, cnt_ref):
-    @pl.loop(0, NBLK)
+    @pl.loop(0, NBLK, unroll=16)
     def _(i):
         cnt_ref[i] = 0
 
-    @pl.loop(0, NBLK)
+    @pl.loop(0, NBLK, unroll=8)
     def _(b):
         o = own_ref[b]
         r = cnt_ref[o]
@@ -415,15 +513,14 @@
 ):
     tz, ty, tx, ix, iy, iz = tables()
     eye = jnp.eye(8, dtype=BF16)
-    sk = jnp.kron(eye, skip_weight.T)
-    w1 = jnp.kron(eye, mlp_in.T)
+    both = jnp.dot(mlp_in, skip_weight, preferred_element_type=F32).astype(BF16)
+    w1 = jnp.concatenate([jnp.kron(eye, mlp_in.T), jnp.kron(eye, both.T)], 0)
     w2 = jnp.kron(eye, mlp_out.T)
     b1 = jnp.tile(mlp_bias, 8)[None, :]
     owner = block_owner.reshape(NBLK)
     send = pack(owner, block_cell, features, point_weights, point_corner.reshape(NBLK, NPTS))
     recv = a2a(send, ("row", "col"))
-    ids = recv[:, 27, 0].astype(jnp.int32)
-    field, zs = scatter(ids, recv, tz)
+    field, zs, ids = scatter(recv, tz)
     zs = a2a(zs, "col")
     ys = y_forward(zs, ty)
     ys = a2a(ys, "row")
@@ -431,7 +528,7 @@
     xs = a2a(xs, "row")
     yi = y_inverse(xs, iy)
     yi = a2a(yi, "col")
-    vals = final(ids, yi, field, recv, iz, sk, w1, b1, w2)
+    vals = final(ids, yi, field, recv, iz, w1, b1, w2)
     vals = a2a(vals, ("row", "col"))
     return unpack(owner, vals)
 

time: 277 us -> 222 us (0.80)
  Pallas kernels: 107 us -> 56.6 us
  other arithmetic: 5.44 us -> 0.92 us
    pallas_call x2, Pallas kernels: 83.6 us -> 37.2 us  [the longest x1 22.9 us: final(): pl.pallas_call(partial(final_kernel, ny=ny, unroll=unroll), out_shape=jax...]
    convert_element_type x1 -> x0, other arithmetic: 5.16 us -> none  [body(): ids = recv[:, 27, 0].astype(jnp.int32)]
where the time goes in v1:
time: 222 us; the launch traced here: 221 us
  blocking collectives  129 us (58%)
  Pallas kernels  56.6 us (25%)
  waiting for transfers between devices  27.1 us (12%)
  starting transfers between devices  3.85 us (2%)
  local copies, waits for them, and re-layouts  3.53 us (2%)
    all_to_all x5, blocking collectives, a2a(): return lax.all_to_all(x, axes, split_axis=0, concat_axis=0, tiled=True)  129 us
    all_to_all x1, waiting for transfers between devices, a2a(): return lax.all_to_all(x, axes, split_axis=0, concat_axis=0, tiled=True)  27.1 us
    pallas_call x1, Pallas kernels, final(): pl.pallas_call(partial(final_kernel, ny=ny, unroll=unroll), out_shape=jax...  22.9 us
    pallas_call x1, Pallas kernels, scatter(): pl.pallas_call(partial(scatter_kernel, unroll=16), out_shape=(jax.ShapeDt...  14.3 us
    pallas_call x1, Pallas kernels, x_mix(): pl.pallas_call(x_kernel, grid=(4,), out_shape=jax.ShapeDtypeStruct((8, 4,...  7 us
  transfers between devices with their start and end apart: 1, of which 1 were waited for; matrix products, arithmetic and copies ran while one was open for 1% of the time, Pallas kernels for 0%

profile of v1, /device:TPU:1, one launch (start us, length us, event | category | flops | bytes accessed | tf_op | source)
XLA Modules:
  0.0 221.0 jit_solution(13955894460246581983)
XLA Ops:
  0.0 3.7 %pack.1 = bf16[256,32,128]{2,1,0:T(8,128)(2,1)} custom-call(s32[128]{0:T(128)} %bitcast.17, s32[128]{0:T(128)} %cell_ref.1, bf16[16,16384]{1,0:T(8,128)(2,1)} %feat_ref.1, bf16[8,16384]{1,0:T(8,128)(2,1)} %w_ref.2, s32[128,128]{1,0:T(8,128)} %bitcast.14), custom_call_target="tpu_custom_call" | custom-call | tf_op jit(solution)/shard_map/pack/pallas_call | solution.py:102
  3.7 41.0 %all_to_all.30.recv_hbm = bf16[256,32,128]{2,1,0:T(8,128)(2,1)} all-to-all(bf16[256,32,128]{2,1,0:T(8,128)(2,1)} %pack.1), channel_id=1, replica_groups=mesh['row'=8,'col'=16] {'row','col'}, dimensions={0} | all-to-all | bytes 4194304 | tf_op jit(solution)/shard_map/all_to_all | solution.py:499
  44.7 14.3 %scatter_z.1 = (bf16[64,256,128]{2,1,0:T(8,128)(2,1)}, bf16[16,8,4,16,128]{4,3,2,1,0:T(8,128)(2,1)}, s32[256]{0:T(256)}) custom-call(bf16[256,32,128]{2,1,0:T(8,128)(2,1)} %all_to_all.30.recv_hbm, bf16[128,256]{1,0:T(8,128)(2,1)} %constant.19.tz_ref), custom_call_target="tpu_custom_call" | custom-call | tf_op jit(solution)/shard_map/scatter_z/pallas_call | solution.py:228
  59.0 31.6 %all_to_all.31.in_ref = bf16[16,8,4,16,128]{4,3,2,1,0:T(8,128)(2,1)} all-to-all(bf16[16,8,4,16,128]{4,3,2,1,0:T(8,128)(2,1)} %get-tuple-element.9), channel_id=1, replica_groups=mesh['row'=8,'col'=16] {'col'}, dimensions={0} | all-to-all | bytes 4194304 | tf_op jit(solution)/shard_map/all_to_all | solution.py:499
  90.6 2.8 %y_forward.1 = bf16[8,4,4,16,128]{4,3,2,1,0:T(8,128)(2,1)} custom-call(bf16[16,8,4,16,128]{4,3,2,1,0:T(8,128)(2,1)} %all_to_all.31.in_ref, bf16[128,512]{1,0:T(8,128)(2,1)} %constant.20.t_ref), custom_call_target="tpu_custom_call" | custom-call | tf_op jit(solution)/shard_map/y_forward/pallas_call | solution.py:265
  93.4 15.7 %all_to_all.32.in_ref = bf16[8,4,4,16,128]{4,3,2,1,0:T(8,128)(2,1)} all-to-all(bf16[8,4,4,16,128]{4,3,2,1,0:T(8,128)(2,1)} %y_forward.1), channel_id=1, replica_groups=mesh['row'=8,'col'=16] {'row'}, dimensions={0} | all-to-all | bytes 1048576 | tf_op jit(solution)/shard_map/all_to_all | solution.py:499
  109.1 7.0 %x_mix.1 = bf16[8,4,4,16,128]{4,3,2,1,0:T(8,128)(2,1)} custom-call(bf16[8,4,4,16,128]{4,3,2,1,0:T(8,128)(2,1)} %all_to_all.32.in_ref, bf16[4,8,16,16,128]{4,3,2,1,0:T(8,128)(2,1)} %w_ref.3, bf16[128,512]{1,0:T(8,128)(2,1)} %constant.21.tx_ref, bf16[512,128]{1,0:T(8,128)(2,1)} %constant.22.ix_ref), custom_call_target="tpu_custom_call" | custom-call | tf_op jit(solution)/shard_map/x_mix/pallas_call | solution.py:314
  116.1 14.5 %all_to_all.33.in_ref = bf16[8,4,4,16,128]{4,3,2,1,0:T(8,128)(2,1)} all-to-all(bf16[8,4,4,16,128]{4,3,2,1,0:T(8,128)(2,1)} %x_mix.1), channel_id=1, replica_groups=mesh['row'=8,'col'=16] {'row'}, dimensions={0} | all-to-all | bytes 1048576 | tf_op jit(solution)/shard_map/all_to_all | solution.py:499
  130.6 3.1 %y_inverse.1 = bf16[16,8,4,16,128]{4,3,2,1,0:T(8,128)(2,1)} custom-call(bf16[8,4,4,16,128]{4,3,2,1,0:T(8,128)(2,1)} %all_to_all.33.in_ref, bf16[512,128]{1,0:T(8,128)(2,1)} %constant.23.t_ref), custom_call_target="tpu_custom_call" | custom-call | tf_op jit(solution)/shard_map/y_inverse/pallas_call | solution.py:347
  133.7 3.8 %all-to-all-start.4 = ((bf16[16,8,4,16,128]{4,3,2,1,0:T(8,128)(2,1)}), bf16[16,8,4,16,128]{4,3,2,1,0:T(8,128)(2,1)S(1)}, u32[]{:S(2)}, u32[]{:S(2)}) async-start(bf16[16,8,4,16,128]{4,3,2,1,0:T(8,128)(2,1)} %y_inverse.1), calls=%async_computation.4 | async-start | bytes 4194304 | tf_op jit(solution)/shard_map/all_to_all | solution.py:499
  137.7 0.2 convolution_convert_fusion
  137.8 0.1 broadcast_multiply_fusion.2
  138.0 0.2 mul.68
  138.2 0.2 mul.71
  138.4 0.1 broadcast_multiply_fusion
  138.5 0.2 mul.75
  138.7 0.8 copy.19.w2_ref
  139.5 0.7 broadcast_in_dim_tile.3.b1_ref
  140.1 0.7 pad_maximum_fusion.w1_ref
  140.9 27.1 %all-to-all-done.4.yi_hbm = bf16[16,8,4,16,128]{4,3,2,1,0:T(8,128)(2,1)S(1)} async-done(((bf16[16,8,4,16,128]{4,3,2,1,0:T(8,128)(2,1)}), bf16[16,8,4,16,128]{4,3,2,1,0:T(8,128)(2,1)S(1)}, u32[]{:S(2)}, u32[]{:S(2)}) %all-to-all-start.4) | async-done | bytes 2097184 | tf_op jit(solution)/shard_map/all_to_all | solution.py:499
  168.0 1.4 copy-done.1
  169.3 22.9 %mlp_gather.1 = bf16[256,16,128]{2,1,0:T(8,128)(2,1)} custom-call(s32[256]{0:T(256)} %get-tuple-element.8.ids_ref, bf16[16,8,4,16,128]{4,3,2,1,0:T(8,128)(2,1)} %copy-done.1, bf16[64,256,128]{2,1,0:T(8,128)(2,1)} %get-tuple-element.10.field_hbm, bf16[256,32,128]{2,1,0:T(8,128)(2,1)} %all_to_all.30.recv_hbm, bf16[256,128]{1,0:T(8,128)(2,1)} %constant.24.iz_ref, ...), custom_call_target="tpu_custom_call" | custom-call | tf_op jit(solution)/shard_map/mlp_gather/pallas_call | solution.py:448
  192.2 26.0 %all_to_all.34.in_ref = bf16[256,16,128]{2,1,0:T(8,128)(2,1)} all-to-all(bf16[256,16,128]{2,1,0:T(8,128)(2,1)} %mlp_gather.1), channel_id=1, replica_groups=mesh['row'=8,'col'=16] {'row','col'}, dimensions={0} | all-to-all | bytes 2097152 | tf_op jit(solution)/shard_map/all_to_all | solution.py:499
  218.2 2.8 %unpack.1 = bf16[16,16384]{1,0:T(8,128)(2,1)} custom-call(s32[128]{0:T(128)} %bitcast.18, bf16[256,16,128]{2,1,0:T(8,128)(2,1)} %all_to_all.34.in_ref), custom_call_target="tpu_custom_call" | custom-call | tf_op jit(solution)/shard_map/unpack/pallas_call | solution.py:488
  (12 shorter events, 0.1 us)
Async XLA Ops:
  0.0 137.7 %copy-start = (bf16[16,16]{1,0:T(8,128)(2,1)S(1)}, bf16[16,16]{1,0:T(8,128)(2,1)}, u32[]{:S(2)}) copy-start(bf16[16,16]{1,0:T(8,128)(2,1)} %param.22) | copy-start | bytes 1540
  133.7 4.0 %copy-start.2 = (bf16[64,16]{0,1:T(8,128)(2,1)S(1)}, bf16[64,16]{0,1:T(8,128)(2,1)}, u32[]{:S(2)}) copy-start(bf16[64,16]{0,1:T(8,128)(2,1)} %param.23) | copy-start | bytes 6148
  133.7 4.7 %copy-start.3 = (bf16[16,64]{1,0:T(8,128)(2,1)S(1)}, bf16[16,64]{1,0:T(8,128)(2,1)}, u32[]{:S(2)}) copy-start(bf16[16,64]{1,0:T(8,128)(2,1)} %param.25) | copy-start | bytes 6148
  133.7 34.3 %all-to-all-start.4 = ((bf16[16,8,4,16,128]{4,3,2,1,0:T(8,128)(2,1)}), bf16[16,8,4,16,128]{4,3,2,1,0:T(8,128)(2,1)S(1)}, u32[]{:S(2)}, u32[]{:S(2)}) async-start(bf16[16,8,4,16,128]{4,3,2,1,0:T(8,128)(2,1)} %y_inverse.1), calls=%async_computation.4 | async-start | bytes 4194304 | tf_op jit(solution)/shard_map/all_to_all | solution.py:499
  137.6 1.9 copy-start.4
  168.0 1.4 copy-start.1

commit v2 on v1

--- a/solution.py
+++ b/solution.py
@@ -50,10 +50,10 @@
     inv = np.stack(
         [np.stack([cf.T, sf.T], -1), np.stack([-sf.T, cf.T], -1)], 1
     )
-    ty = fwd.reshape(COLS, 16, 2, ROWS, 8, 2).transpose(3, 5, 4, 0, 2, 1).reshape(128, 512)
-    tx = fwd.reshape(ROWS, 4, 8, 2, MODES, 2).transpose(5, 4, 0, 1, 3, 2).reshape(128, 512)
-    ix = inv.reshape(MODES, 2, ROWS, 4, 8, 2).transpose(2, 3, 5, 4, 1, 0).reshape(512, 128)
-    iy = inv.reshape(ROWS, 8, 2, COLS, 16, 2).transpose(3, 5, 4, 0, 2, 1).reshape(512, 128)
+    ty = fwd.reshape(COLS, 16, 2, 4, 16, 2).transpose(3, 5, 4, 0, 2, 1).reshape(128, 512)
+    tx = fwd.reshape(ROWS, 2, 2, 8, 2, MODES, 2).transpose(6, 5, 0, 1, 4, 2, 3).reshape(128, 512)
+    ix = inv.reshape(MODES, 2, ROWS, 2, 2, 8, 2).transpose(2, 3, 6, 4, 5, 1, 0).reshape(512, 128)
+    iy = inv.reshape(4, 16, 2, COLS, 16, 2).transpose(3, 5, 4, 0, 2, 1).reshape(512, 128)
     a = np.where(np.arange(MODES) == 0, 1.0, 2.0)[None, :]
     iz = np.stack([a * cz, -a * sz], -1).reshape(GRID, 2 * MODES)
     return [jnp.asarray(t.astype(np.float32)).astype(BF16) for t in (tz, ty, tx, ix, iy, iz)]
@@ -138,6 +138,13 @@
     return jnp.concatenate(halves, 1)
 
 
+def split_lanes(a, b):
+    low = lax.broadcasted_iota(jnp.int32, a.shape, a.ndim - 1) < 64
+    first = jnp.where(low, a, pltpu.roll(b, 64, a.ndim - 1))
+    second = jnp.where(low, pltpu.roll(a, 64, a.ndim - 1), b)
+    return first, second
+
+
 def scatter_kernel(
     recv_hbm, tz_ref, field_hbm, out_hbm, ids_ref,
     recv_ref, g_ref, z_ref, field_ref, out_ref, in_sem, field_sem, out_sem, *, unroll
@@ -167,11 +174,17 @@
                 tail = recv_ref[s, 16:32, :].astype(F32)
                 basis = yz_basis(tail)
                 feat = recv_ref[s, 0:16, :].astype(F32)
-                vx = jnp.broadcast_to(tail[8:9, :], (16, NPTS))
-                zf = jnp.zeros((16, NPTS), BF16)
-                sel = [jnp.where(vx == float(x), feat, 0.0).astype(BF16) for x in range(7)]
+                vx = jnp.broadcast_to(tail[8:9, :], (8, NPTS))
+                zf = jnp.zeros((8, NPTS), F32)
+                low, high = [], []
+                for ch in range(2):
+                    half = feat[ch * 8 : ch * 8 + 8]
+                    sel = [jnp.where(vx == float(x), half, 0.0) for x in range(7)]
+                    low += sel + [zf]
+                    high += [zf] + sel
                 lhs = jnp.concatenate(
-                    [jnp.concatenate(sel + [zf], 0), jnp.concatenate([zf] + sel, 0)], 1
+                    [jnp.concatenate(low, 0).astype(BF16), jnp.concatenate(high, 0).astype(BF16)],
+                    1,
                 )
                 res = mm(basis, lhs, NT)
                 b = jnp.clip(tail[11, 0].astype(jnp.int32) - 1, 0, 255)
@@ -184,8 +197,10 @@
         at = pl.ds(q * 8, 8)
         return pltpu.make_async_copy(field_ref.at[at], field_hbm.at[at], field_sem.at[q])
 
-    def put_out(s):
-        return pltpu.make_async_copy(out_ref.at[s], out_hbm.at[s], out_sem.at[s])
+    def put_out(s, r):
+        return pltpu.make_async_copy(
+            out_ref.at[s, r], out_hbm.at[r * COLS + s], out_sem.at[s, r]
+        )
 
     @pl.loop(0, 8)
     def _(q):
@@ -206,11 +221,17 @@
 
     @pl.loop(0, 16)
     def _(s):
-        for k in range(8):
-            for bx in range(4):
-                at = pl.multiple_of(s * 128 + k * 16, 16)
-                out_ref[s, k, bx] = z_ref[bx, pl.ds(at, 16), :].astype(BF16)
-        put_out(s).start()
+        for kz in range(4):
+            for ri in range(2):
+                at = pl.multiple_of(s * 128 + kz * 32 + ri * 16, 16)
+                for p in range(2):
+                    pair = split_lanes(
+                        z_ref[2 * p, pl.ds(at, 16), :], z_ref[2 * p + 1, pl.ds(at, 16), :]
+                    )
+                    for ch in range(2):
+                        out_ref[s, 2 * kz + ch, ri, p] = pair[ch].astype(BF16)
+        for r in range(8):
+            put_out(s, r).start()
 
     @pl.loop(0, 8)
     def _(q):
@@ -218,7 +239,8 @@
 
     @pl.loop(0, 16)
     def _(s):
-        put_out(s).wait()
+        for r in range(8):
+            put_out(s, r).wait()
 
 
 def scatter(recv, tz):
@@ -229,7 +251,7 @@
         partial(scatter_kernel, unroll=16),
         out_shape=(
             jax.ShapeDtypeStruct((64, GRID, 128), BF16),
-            jax.ShapeDtypeStruct((16, 8, 4, 16, 128), BF16),
+            jax.ShapeDtypeStruct((128, 2, 2, 16, 128), BF16),
             jax.ShapeDtypeStruct((NSLOT,), jnp.int32),
         ),
         in_specs=[hbm, vmem],
@@ -239,116 +261,152 @@
             pltpu.VMEM((256, 64, 128), F32),
             pltpu.VMEM((4, 2048, 128), F32),
             pltpu.VMEM((64, GRID, 128), BF16),
-            pltpu.VMEM((16, 8, 4, 16, 128), BF16),
+            pltpu.VMEM((16, 8, 2, 2, 16, 128), BF16),
             pltpu.SemaphoreType.DMA((4,)),
             pltpu.SemaphoreType.DMA((8,)),
-            pltpu.SemaphoreType.DMA((16,)),
+            pltpu.SemaphoreType.DMA((16, 8)),
         ],
         name="scatter_z",
     )(recv, tz)
 
 
-def y_kernel(in_ref, t_ref, out_ref):
-    t = t_ref[...]
-    for kz in range(4):
-        for h in range(2):
-            rhs = jnp.concatenate(
-                [in_ref[:, 2 * kz : 2 * kz + 2, 2 * h + e].reshape(512, 128) for e in range(2)], 1
-            )
-            res = mm(t, rhs).astype(BF16)
-            for r in range(8):
-                for e in range(2):
-                    out_ref[r, kz, 2 * h + e] = res[r * 16 : r * 16 + 16, e * 128 : e * 128 + 128]
-
-
-def y_forward(zs, ty):
-    return pl.pallas_call(
-        y_kernel,
-        out_shape=jax.ShapeDtypeStruct((8, 4, 4, 16, 128), BF16),
-        name="y_forward",
-    )(zs, ty)
-
-
-def block_transpose(x):
+def group_transpose(x):
+    n = x.shape[0]
+    low, high = split_lanes(x[:, 0:8], x[:, 8:16])
+    x = jnp.concatenate([low, high], 0)
     si = lax.broadcasted_iota(jnp.int32, x.shape, 1)
-    gi = lax.broadcasted_iota(jnp.int32, x.shape, 2) // 16
+    gi = lax.broadcasted_iota(jnp.int32, x.shape, 2) // 8
     for k in range(3):
         d = 1 << k
         mi = (si // d) % 2
         mg = (gi // d) % 2
-        up = pltpu.roll(pltpu.roll(x, 8 - d, 1), 16 * d, 2)
-        if k == 2:
-            x = jnp.where(mi == mg, x, up)
-        else:
-            down = pltpu.roll(pltpu.roll(x, d, 1), 128 - 16 * d, 2)
-            x = jnp.where(mi == mg, x, jnp.where(mi < mg, up, down))
-    return x
-
-
-def x_kernel(in_ref, w_ref, tx_ref, ix_ref, out_ref):
-    data = in_ref[...].astype(F32).reshape(64, 8, 128)
-    data = block_transpose(data).reshape(512, 128).astype(BF16)
-    spec = mm(tx_ref[...], data).T.astype(BF16).astype(F32)
-    swapped = pltpu.roll(spec, 64, 1)
+        up = pltpu.roll(pltpu.roll(x, 8 - d, 1), 8 * d, 2)
+        down = pltpu.roll(pltpu.roll(x, d, 1), 128 - 8 * d, 2)
+        x = jnp.where(mi == mg, x, jnp.where(mi < mg, up, down))
+    return jnp.concatenate([x[:n], x[n:]], 1)
+
+
+def yx_kernel(in_hbm, ty_ref, tx_ref, out_ref, in_ref, v_ref, sem):
+    def get(r):
+        at = pl.ds(r * COLS, COLS)
+        return pltpu.make_async_copy(in_hbm.at[at], in_ref.at[at], sem.at[r])
+
+    for r in range(8):
+        get(r).start()
+
+    @pl.loop(0, 8)
+    def _(r):
+        get(r).wait()
+        at = pl.ds(r * COLS, COLS)
+        rhs = jnp.concatenate([in_ref[at, :, p].reshape(512, 128) for p in range(2)], 1)
+        res = mm(ty_ref[...], rhs)
+        for p in range(2):
+            tiles = group_transpose(res[:, p * 128 : p * 128 + 128].reshape(8, 16, 128))
+            tiles = tiles.reshape(4, 32, 128).astype(BF16)
+            to = pl.multiple_of(r * 64 + p * 32, 32)
+            for g in range(4):
+                v_ref[g, pl.ds(to, 32), :] = tiles[g]
+
+    for g in range(4):
+        spec = mm(tx_ref[...], v_ref[g]).T.astype(BF16)
+        out_ref[2 * g] = spec[0:64]
+        out_ref[2 * g + 1] = spec[64:128]
+
+
+def yx_forward(zs, ty, tx):
+    vmem = pl.BlockSpec(memory_space=pltpu.VMEM)
+    hbm = pl.BlockSpec(memory_space=pl.ANY)
+    return pl.pallas_call(
+        yx_kernel,
+        out_shape=jax.ShapeDtypeStruct((8, 64, 128), BF16),
+        in_specs=[hbm, vmem, vmem],
+        out_specs=vmem,
+        scratch_shapes=[
+            pltpu.VMEM((128, 2, 2, 16, 128), BF16),
+            pltpu.VMEM((4, 512, 128), BF16),
+            pltpu.SemaphoreType.DMA((8,)),
+        ],
+        name="yx_forward",
+    )(zs, ty, tx)
+
+
+def mix_kernel(in_ref, w_ref, out_ref):
     lane = lax.broadcasted_iota(jnp.int32, (16, 128), 1)
-    parts = []
+    halves = [[], []]
+    spec = [in_ref[ch].astype(F32) for ch in range(2)]
+    swapped = [pltpu.roll(x, 64, 1) for x in spec]
     for ky in range(8):
         a1 = jnp.zeros((16, 128), F32)
         a2 = jnp.zeros((16, 128), F32)
         for c in range(CH):
             w = w_ref[0, ky, c].astype(F32)
-            at = ky * 16 + c
-            a1 = a1 + spec[at : at + 1, :] * w
-            a2 = a2 + swapped[at : at + 1, :] * w
-        parts.append(
-            jnp.where(lane < 64, a1 - pltpu.roll(a1, 64, 1), a2 + pltpu.roll(a2, 64, 1))
+            at = ky * 8 + c % 8
+            a1 = a1 + spec[c // 8][at : at + 1, :] * w
+            a2 = a2 + swapped[c // 8][at : at + 1, :] * w
+        res = jnp.where(lane < 64, a1 - pltpu.roll(a1, 64, 1), a2 + pltpu.roll(a2, 64, 1))
+        for h in range(2):
+            halves[h].append(res[h * 8 : h * 8 + 8])
+    for h in range(2):
+        out_ref[h] = jnp.concatenate(halves[h], 0).astype(BF16)
+
+
+def mix(spec, weight):
+    return pl.pallas_call(
+        mix_kernel,
+        grid=(4,),
+        out_shape=jax.ShapeDtypeStruct((8, 64, 128), BF16),
+        in_specs=[
+            pl.BlockSpec((2, 64, 128), lambda k: (k, 0, 0)),
+            pl.BlockSpec((1, 8, 16, 16, 128), lambda k: (k, 0, 0, 0, 0)),
+        ],
+        out_specs=pl.BlockSpec((2, 64, 128), lambda k: (k, 0, 0)),
+        name="mix",
+    )(spec, weight)
+
+
+def xy_kernel(in_ref, ix_ref, iy_ref, out_hbm, u_ref, out_ref, sem):
+    def put(r):
+        at = pl.ds(r * COLS, COLS)
+        return pltpu.make_async_copy(out_ref.at[at], out_hbm.at[at], sem.at[r])
+
+    @pl.loop(0, 4)
+    def _(g):
+        rhs = in_ref[pl.ds(2 * g, 2)].reshape(128, 128)
+        xi = group_transpose(mm(ix_ref[...], rhs, NT).reshape(32, 16, 128))
+        u_ref[g] = xi.astype(BF16)
+
+    @pl.loop(0, 8)
+    def _(r):
+        rhs = jnp.concatenate(
+            [u_ref[:, pl.ds(r * 4 + p * 2, 2)].reshape(128, 128) for p in range(2)], 1
         )
-    mixed = jnp.concatenate(parts, 0).astype(BF16)
-    xi = mm(ix_ref[...], mixed, NT)
-    xi = block_transpose(xi.reshape(64, 8, 128))
-    out_ref[...] = xi.reshape(8, 1, 4, 16, 128).astype(BF16)
-
-
-def x_mix(ys, weight, tx, ix):
-    whole = lambda k: (0, 0)
+        res = mm(iy_ref[...], rhs).astype(BF16)
+        for s in range(16):
+            for ri in range(2):
+                at = s * 32 + ri * 16
+                for p in range(2):
+                    out_ref[r * COLS + s, ri, p] = res[at : at + 16, p * 128 : p * 128 + 128]
+        put(r).start()
+
+    for r in range(8):
+        put(r).wait()
+
+
+def xy_inverse(mixed, ix, iy):
+    vmem = pl.BlockSpec(memory_space=pltpu.VMEM)
+    hbm = pl.BlockSpec(memory_space=pl.ANY)
     return pl.pallas_call(
-        x_kernel,
-        grid=(4,),
-        out_shape=jax.ShapeDtypeStruct((8, 4, 4, 16, 128), BF16),
-        in_specs=[
-            pl.BlockSpec((8, 1, 4, 16, 128), lambda k: (0, k, 0, 0, 0)),
-            pl.BlockSpec((1, 8, 16, 16, 128), lambda k: (k, 0, 0, 0, 0)),
-            pl.BlockSpec((128, 512), whole),
-            pl.BlockSpec((512, 128), whole),
+        xy_kernel,
+        out_shape=jax.ShapeDtypeStruct((128, 2, 2, 16, 128), BF16),
+        in_specs=[vmem, vmem, vmem],
+        out_specs=hbm,
+        scratch_shapes=[
+            pltpu.VMEM((4, 32, 16, 128), BF16),
+            pltpu.VMEM((128, 2, 2, 16, 128), BF16),
+            pltpu.SemaphoreType.DMA((8,)),
         ],
-        out_specs=pl.BlockSpec((8, 1, 4, 16, 128), lambda k: (0, k, 0, 0, 0)),
-        name="x_mix",
-    )(ys, weight, tx, ix)
-
-
-def yi_kernel(in_ref, t_ref, out_ref):
-    t = t_ref[...]
-    for kz in range(4):
-        for h in range(2):
-            rhs = jnp.concatenate(
-                [in_ref[:, kz, 2 * h + e].reshape(128, 128) for e in range(2)], 1
-            )
-            res = mm(t, rhs).astype(BF16)
-            for s in range(16):
-                for ri in range(2):
-                    at = s * 32 + ri * 16
-                    for e in range(2):
-                        out_ref[s, 2 * kz + ri, 2 * h + e] = res[
-                            at : at + 16, e * 128 : e * 128 + 128
-                        ]
-
-
-def y_inverse(xs, iy):
-    return pl.pallas_call(
-        yi_kernel,
-        out_shape=jax.ShapeDtypeStruct((16, 8, 4, 16, 128), BF16),
-        name="y_inverse",
-    )(xs, iy)
+        name="xy_inverse",
+    )(mixed, ix, iy)
 
 
 def gelu(x):
@@ -364,8 +422,9 @@
     yi_ref, field_ref, tail_ref, out_ref, y_ref, x_ref, l_ref,
     yi_sem, field_sem, tail_sem, out_sem, *, ny, unroll
 ):
-    def get_yi(s):
-        return pltpu.make_async_copy(yi_hbm.at[s], yi_ref.at[s], yi_sem.at[s])
+    def get_yi(r):
+        at = pl.ds(r * COLS, COLS)
+        return pltpu.make_async_copy(yi_hbm.at[at], yi_ref.at[at], yi_sem.at[r])
 
     def get_field(i):
         at = pl.ds(i * ny, ny)
@@ -377,9 +436,9 @@
 
     get_tail = pltpu.make_async_copy(recv_hbm.at[:, 16:32], tail_ref, tail_sem)
 
-    @pl.loop(0, 16)
-    def _(s):
-        get_yi(s).start()
+    @pl.loop(0, 8)
+    def _(r):
+        get_yi(r).start()
 
     @pl.loop(0, 64 // ny)
     def _(i):
@@ -387,13 +446,22 @@
 
     get_tail.start()
 
-    @pl.loop(0, 16)
-    def _(s):
-        get_yi(s).wait()
-        for k in range(8):
-            for bx in range(4):
-                at = pl.multiple_of(s * 128 + k * 16, 16)
-                y_ref[bx, pl.ds(at, 16), :] = yi_ref[s, k, bx].astype(F32)
+    @pl.loop(0, 4)
+    def _(kz):
+        get_yi(2 * kz).wait()
+        get_yi(2 * kz + 1).wait()
+
+        @pl.loop(0, 16)
+        def _(s):
+            for ri in range(2):
+                at = pl.multiple_of(s * 128 + kz * 32 + ri * 16, 16)
+                for p in range(2):
+                    pair = split_lanes(
+                        yi_ref[kz * 32 + s, ri, p].astype(F32),
+                        yi_ref[kz * 32 + 16 + s, ri, p].astype(F32),
+                    )
+                    for e in range(2):
+                        y_ref[2 * p + e, pl.ds(at, 16), :] = pair[e]
 
     @pl.loop(0, 64 // ny)
     def _(i):
@@ -451,14 +519,14 @@
         in_specs=[smem, hbm, hbm, hbm, vmem, vmem, vmem, vmem],
         out_specs=hbm,
         scratch_shapes=[
-            pltpu.VMEM((16, 8, 4, 16, 128), BF16),
+            pltpu.VMEM((128, 2, 2, 16, 128), BF16),
             pltpu.VMEM((64, GRID, 128), BF16),
             pltpu.VMEM((NSLOT, 16, NPTS), BF16),
             pltpu.VMEM((NSLOT, 16, NPTS), BF16),
             pltpu.VMEM((4, 2048, 128), F32),
             pltpu.VMEM((ny * GRID, 256), BF16),
             pltpu.VMEM((64, GRID, 128), F32),
-            pltpu.SemaphoreType.DMA((16,)),
+            pltpu.SemaphoreType.DMA((8,)),
             pltpu.SemaphoreType.DMA((64 // ny,)),
             pltpu.SemaphoreType.DMA,
             pltpu.SemaphoreType.DMA((NSLOT // unroll,)),
@@ -514,20 +582,18 @@
     tz, ty, tx, ix, iy, iz = tables()
     eye = jnp.eye(8, dtype=BF16)
     both = jnp.dot(mlp_in, skip_weight, preferred_element_type=F32).astype(BF16)
-    w1 = jnp.concatenate([jnp.kron(eye, mlp_in.T), jnp.kron(eye, both.T)], 0)
+    w1 = jnp.stack([jnp.kron(eye, mlp_in.T), jnp.kron(eye, both.T)], 0)
+    w1 = w1.reshape(2, 8, 2, 8, 512).transpose(0, 2, 1, 3, 4).reshape(256, 512)
     w2 = jnp.kron(eye, mlp_out.T)
     b1 = jnp.tile(mlp_bias, 8)[None, :]
     owner = block_owner.reshape(NBLK)
     send = pack(owner, block_cell, features, point_weights, point_corner.reshape(NBLK, NPTS))
     recv = a2a(send, ("row", "col"))
     field, zs, ids = scatter(recv, tz)
-    zs = a2a(zs, "col")
-    ys = y_forward(zs, ty)
-    ys = a2a(ys, "row")
-    xs = x_mix(ys, spec_weight, tx, ix)
-    xs = a2a(xs, "row")
-    yi = y_inverse(xs, iy)
-    yi = a2a(yi, "col")
+    zs = a2a(zs, ("row", "col"))
+    spec = a2a(yx_forward(zs, ty, tx), "row")
+    mixed = a2a(mix(spec, spec_weight), "row")
+    yi = a2a(xy_inverse(mixed, ix, iy), ("row", "col"))
     vals = final(ids, yi, field, recv, iz, w1, b1, w2)
     vals = a2a(vals, ("row", "col"))
     return unpack(owner, vals)

time: 222 us -> 226 us (1.018)
  Pallas kernels: 56.6 us -> 67.1 us
  blocking collectives: 129 us -> 122 us
    all_to_all x5, blocking collectives: 129 us -> 122 us  [a2a(): return lax.all_to_all(x, axes, split_axis=0, concat_axis=0, tiled=True)]
    pallas_call x1, Pallas kernels: 22.9 us -> 27.2 us  [final(): pl.pallas_call(partial(final_kernel, ny=ny, unroll=unroll), out_shape=jax...]
    pallas_call x3, Pallas kernels: 13 us -> 16.8 us  [the longest x1 7.08 us: yx_forward(): pl.pallas_call(yx_kernel, out_shape=jax.ShapeDtypeStruct((8, 64, 128), BF...]
    pallas_call x1, Pallas kernels: 14.3 us -> 16.6 us  [scatter(): pl.pallas_call(partial(scatter_kernel, unroll=16), out_shape=(jax.ShapeDt...]
where the time goes in v2:
time: 226 us; the launch traced here: 225 us
  blocking collectives  122 us (54%)
  Pallas kernels  67.1 us (30%)
  waiting for transfers between devices  26.2 us (12%)
  starting transfers between devices  4.47 us (2%)
  local copies, waits for them, and re-layouts  3.5 us (2%)
    all_to_all x5, blocking collectives, a2a(): return lax.all_to_all(x, axes, split_axis=0, concat_axis=0, tiled=True)  122 us
    pallas_call x1, Pallas kernels, final(): pl.pallas_call(partial(final_kernel, ny=ny, unroll=unroll), out_shape=jax...  27.2 us
    all_to_all x1, waiting for transfers between devices, a2a(): return lax.all_to_all(x, axes, split_axis=0, concat_axis=0, tiled=True)  26.2 us
    pallas_call x1, Pallas kernels, scatter(): pl.pallas_call(partial(scatter_kernel, unroll=16), out_shape=(jax.ShapeDt...  16.6 us
    pallas_call x1, Pallas kernels, yx_forward(): pl.pallas_call(yx_kernel, out_shape=jax.ShapeDtypeStruct((8, 64, 128), BF...  7.08 us
    pallas_call x1, Pallas kernels, xy_inverse(): pl.pallas_call(xy_kernel, out_shape=jax.ShapeDtypeStruct((128, 2, 2, 16,...  5.66 us
  transfers between devices with their start and end apart: 1, of which 1 were waited for; matrix products, arithmetic and copies ran while one was open for 1% of the time, Pallas kernels for 0%

profile of v2, /device:TPU:1, one launch (start us, length us, event | category | flops | bytes accessed | tf_op | source)
XLA Modules:
  0.0 224.8 jit_solution(14147559788716808226)
XLA Ops:
  0.0 3.7 %pack.1 = bf16[256,32,128]{2,1,0:T(8,128)(2,1)} custom-call(s32[128]{0:T(128)} %bitcast.17, s32[128]{0:T(128)} %cell_ref.1, bf16[16,16384]{1,0:T(8,128)(2,1)} %feat_ref.1, bf16[8,16384]{1,0:T(8,128)(2,1)} %w_ref.2, s32[128,128]{1,0:T(8,128)} %bitcast.14), custom_call_target="tpu_custom_call" | custom-call | tf_op jit(solution)/shard_map/pack/pallas_call | solution.py:102
  3.7 41.0 %all_to_all.30.recv_hbm = bf16[256,32,128]{2,1,0:T(8,128)(2,1)} all-to-all(bf16[256,32,128]{2,1,0:T(8,128)(2,1)} %pack.1), channel_id=1, replica_groups=mesh['row'=8,'col'=16] {'row','col'}, dimensions={0} | all-to-all | bytes 4194304 | tf_op jit(solution)/shard_map/all_to_all | solution.py:567
  44.7 16.6 %scatter_z.1 = (bf16[64,256,128]{2,1,0:T(8,128)(2,1)}, bf16[128,2,2,16,128]{4,3,2,1,0:T(8,128)(2,1)}, s32[256]{0:T(256)}) custom-call(bf16[256,32,128]{2,1,0:T(8,128)(2,1)} %all_to_all.30.recv_hbm, bf16[128,256]{1,0:T(8,128)(2,1)} %constant.19.tz_ref), custom_call_target="tpu_custom_call" | custom-call | tf_op jit(solution)/shard_map/scatter_z/pallas_call | solution.py:250
  61.3 35.4 %all_to_all.31.in_hbm = bf16[128,2,2,16,128]{4,3,2,1,0:T(8,128)(2,1)} all-to-all(bf16[128,2,2,16,128]{4,3,2,1,0:T(8,128)(2,1)} %get-tuple-element.9), channel_id=1, replica_groups=mesh['row'=8,'col'=16] {'row','col'}, dimensions={0} | all-to-all | bytes 4194304 | tf_op jit(solution)/shard_map/all_to_all | solution.py:567
  96.7 7.1 %yx_forward.1 = bf16[8,64,128]{2,1,0:T(8,128)(2,1)} custom-call(bf16[128,2,2,16,128]{4,3,2,1,0:T(8,128)(2,1)} %all_to_all.31.in_hbm, bf16[128,512]{1,0:T(8,128)(2,1)} %constant.20.ty_ref, bf16[128,512]{1,0:T(8,128)(2,1)} %constant.21.tx_ref), custom_call_target="tpu_custom_call" | custom-call | tf_op jit(solution)/shard_map/yx_forward/pallas_call | solution.py:319
  103.7 10.6 %all_to_all.32.in_ref = bf16[8,64,128]{2,1,0:T(8,128)(2,1)} all-to-all(bf16[8,64,128]{2,1,0:T(8,128)(2,1)} %yx_forward.1), channel_id=1, replica_groups=mesh['row'=8,'col'=16] {'row'}, dimensions={0} | all-to-all | bytes 262144 | tf_op jit(solution)/shard_map/all_to_all | solution.py:567
  114.4 4.1 %mix.1 = bf16[8,64,128]{2,1,0:T(8,128)(2,1)} custom-call(bf16[8,64,128]{2,1,0:T(8,128)(2,1)} %all_to_all.32.in_ref, bf16[4,8,16,16,128]{4,3,2,1,0:T(8,128)(2,1)} %w_ref.3), custom_call_target="tpu_custom_call" | custom-call | tf_op jit(solution)/shard_map/mix/pallas_call | solution.py:354
  118.4 10.1 %all_to_all.33.in_ref = bf16[8,64,128]{2,1,0:T(8,128)(2,1)} all-to-all(bf16[8,64,128]{2,1,0:T(8,128)(2,1)} %mix.1), channel_id=1, replica_groups=mesh['row'=8,'col'=16] {'row'}, dimensions={0} | all-to-all | bytes 262144 | tf_op jit(solution)/shard_map/all_to_all | solution.py:567
  128.5 5.7 %xy_inverse.1 = bf16[128,2,2,16,128]{4,3,2,1,0:T(8,128)(2,1)} custom-call(bf16[8,64,128]{2,1,0:T(8,128)(2,1)} %all_to_all.33.in_ref, bf16[512,128]{1,0:T(8,128)(2,1)} %constant.22.ix_ref, bf16[512,128]{1,0:T(8,128)(2,1)} %constant.23.iy_ref), custom_call_target="tpu_custom_call" | custom-call | tf_op jit(solution)/shard_map/xy_inverse/pallas_call | solution.py:398
  134.2 4.5 %all-to-all-start.4 = ((bf16[128,2,2,16,128]{4,3,2,1,0:T(8,128)(2,1)}), bf16[128,2,2,16,128]{4,3,2,1,0:T(8,128)(2,1)S(1)}, u32[]{:S(2)}, u32[]{:S(2)}) async-start(bf16[128,2,2,16,128]{4,3,2,1,0:T(8,128)(2,1)} %xy_inverse.1), calls=%async_computation.4 | async-start | bytes 4194304 | tf_op jit(solution)/shard_map/all_to_all | solution.py:567
  138.9 0.1 mul.90
  139.0 0.2 convolution_convert_fusion
  139.2 0.1 mul.97
  139.3 0.1 mul.93
  139.4 0.1 broadcast_multiply_fusion
  139.5 0.2 mul.103
  139.7 0.8 copy.19.w2_ref
  140.5 0.7 broadcast_in_dim_tile.3.b1_ref
  141.2 0.7 pad_maximum_fusion
  141.9 26.2 %all-to-all-done.4.yi_hbm = bf16[128,2,2,16,128]{4,3,2,1,0:T(8,128)(2,1)S(1)} async-done(((bf16[128,2,2,16,128]{4,3,2,1,0:T(8,128)(2,1)}), bf16[128,2,2,16,128]{4,3,2,1,0:T(8,128)(2,1)S(1)}, u32[]{:S(2)}, u32[]{:S(2)}) %all-to-all-start.4) | async-done | bytes 2097184 | tf_op jit(solution)/shard_map/all_to_all | solution.py:567
  168.1 1.4 copy-done.1
  169.5 27.2 %mlp_gather.1 = bf16[256,16,128]{2,1,0:T(8,128)(2,1)} custom-call(s32[256]{0:T(256)} %get-tuple-element.8.ids_ref, bf16[128,2,2,16,128]{4,3,2,1,0:T(8,128)(2,1)} %copy-done.1, bf16[64,256,128]{2,1,0:T(8,128)(2,1)} %get-tuple-element.10.field_hbm, bf16[256,32,128]{2,1,0:T(8,128)(2,1)} %all_to_all.30.recv_hbm, bf16[256,128]{1,0:T(8,128)(2,1)} %constant.24.iz_ref, ...), custom_call_target="tpu_custom_call" | custom-call | tf_op jit(solution)/shard_map/mlp_gather/pallas_call | solution.py:516
  196.7 25.3 %all_to_all.34.in_ref = bf16[256,16,128]{2,1,0:T(8,128)(2,1)} all-to-all(bf16[256,16,128]{2,1,0:T(8,128)(2,1)} %mlp_gather.1), channel_id=1, replica_groups=mesh['row'=8,'col'=16] {'row','col'}, dimensions={0} | all-to-all | bytes 2097152 | tf_op jit(solution)/shard_map/all_to_all | solution.py:567
  222.0 2.8 %unpack.1 = bf16[16,16384]{1,0:T(8,128)(2,1)} custom-call(s32[128]{0:T(128)} %bitcast.18, bf16[256,16,128]{2,1,0:T(8,128)(2,1)} %all_to_all.34.in_ref), custom_call_target="tpu_custom_call" | custom-call | tf_op jit(solution)/shard_map/unpack/pallas_call | solution.py:556
  (16 shorter events, 0.2 us)
Async XLA Ops:
  0.0 139.0 %copy-start = (bf16[16,16]{1,0:T(8,128)(2,1)S(1)}, bf16[16,16]{1,0:T(8,128)(2,1)}, u32[]{:S(2)}) copy-start(bf16[16,16]{1,0:T(8,128)(2,1)} %param.22) | copy-start | bytes 1540
  134.2 4.8 %copy-start.2 = (bf16[64,16]{0,1:T(8,128)(2,1)S(1)}, bf16[64,16]{0,1:T(8,128)(2,1)}, u32[]{:S(2)}) copy-start(bf16[64,16]{0,1:T(8,128)(2,1)} %param.23) | copy-start | bytes 6148
  134.2 5.2 %copy-start.3 = (bf16[16,64]{1,0:T(8,128)(2,1)S(1)}, bf16[16,64]{1,0:T(8,128)(2,1)}, u32[]{:S(2)}) copy-start(bf16[16,64]{1,0:T(8,128)(2,1)} %param.25) | copy-start | bytes 6148
  134.2 6.2 %copy-start.4 = (f32[64]{0:T(128)S(1)}, f32[64]{0:T(128)}, u32[]{:S(2)}) copy-start(f32[64]{0:T(128)} %param.24) | copy-start | bytes 772
  134.2 33.9 %all-to-all-start.4 = ((bf16[128,2,2,16,128]{4,3,2,1,0:T(8,128)(2,1)}), bf16[128,2,2,16,128]{4,3,2,1,0:T(8,128)(2,1)S(1)}, u32[]{:S(2)}, u32[]{:S(2)}) async-start(bf16[128,2,2,16,128]{4,3,2,1,0:T(8,128)(2,1)} %xy_inverse.1), calls=%async_computation.4 | async-start | bytes 4194304 | tf_op jit(solution)/shard_map/all_to_all | solution.py:567
  168.1 1.4 copy-start.1

commit v3 on v2

--- a/solution.py
+++ b/solution.py
@@ -30,6 +30,10 @@
     return lax.dot_general(a, b, dims, preferred_element_type=F32)
 
 
+ROW_IN = np.array([2 * lo + hi for hi in range(2) for lo in range(8)])
+ROW_OUT = np.array([2 * ((-t) % 8) + v for v in range(2) for t in range(8)])
+
+
 def _freqs():
     j = np.arange(MODES)
     return np.where(j < MODES // 2, j, GRID - MODES + j)
@@ -50,10 +54,14 @@
     inv = np.stack(
         [np.stack([cf.T, sf.T], -1), np.stack([-sf.T, cf.T], -1)], 1
     )
-    ty = fwd.reshape(COLS, 16, 2, 4, 16, 2).transpose(3, 5, 4, 0, 2, 1).reshape(128, 512)
-    tx = fwd.reshape(ROWS, 2, 2, 8, 2, MODES, 2).transpose(6, 5, 0, 1, 4, 2, 3).reshape(128, 512)
-    ix = inv.reshape(MODES, 2, ROWS, 2, 2, 8, 2).transpose(2, 3, 6, 4, 5, 1, 0).reshape(512, 128)
-    iy = inv.reshape(4, 16, 2, COLS, 16, 2).transpose(3, 5, 4, 0, 2, 1).reshape(512, 128)
+    ty = fwd.reshape(COLS, 16, 2, 4, 16, 2)[:, :, :, :, ROW_IN]
+    ty = ty.transpose(3, 5, 4, 0, 2, 1).reshape(128, 512)
+    tx = fwd.reshape(ROWS, 2, 16, 2, MODES, 2)[:, :, ROW_OUT]
+    tx = tx.transpose(5, 4, 0, 1, 3, 2).reshape(128, 512)
+    ix = inv.reshape(MODES, 2, ROWS, 2, 16, 2)[:, :, :, :, ROW_IN]
+    ix = ix.transpose(2, 3, 5, 4, 1, 0).reshape(512, 128)
+    iy = inv.reshape(4, 16, 2, COLS, 16, 2)[:, ROW_OUT]
+    iy = iy.transpose(3, 5, 4, 0, 2, 1).reshape(512, 128)
     a = np.where(np.arange(MODES) == 0, 1.0, 2.0)[None, :]
     iz = np.stack([a * cz, -a * sz], -1).reshape(GRID, 2 * MODES)
     return [jnp.asarray(t.astype(np.float32)).astype(BF16) for t in (tz, ty, tx, ix, iy, iz)]
@@ -63,27 +71,31 @@
     return ((v.astype(F32) + 0.5) * (1.0 / d)).astype(jnp.int32)
 
 
-def pack_kernel(own_ref, cell_ref, feat_ref, w_ref, corner_ref, send_ref, cnt_ref):
-    zero = jnp.zeros((8, 32, NPTS), BF16)
-
-    @pl.loop(0, NSLOT // 8)
+def pack_kernel(
+    own_ref, cell_ref, feat_ref, w_ref, corner_ref, send_ref, slot_ref, cnt_ref, head_ref
+):
+    zero = jnp.zeros((8, 56, NPTS), BF16)
+
+    @pl.loop(0, NBLK // 8)
     def _(i):
         send_ref[pl.ds(i * 8, 8)] = zero
+        head_ref[pl.ds(i * 8, 8)] = jnp.zeros((8, 8, NPTS), F32)
 
     @pl.loop(0, NBLK, unroll=16)
     def _(i):
         cnt_ref[i] = 0
 
-    row = lax.broadcasted_iota(jnp.int32, (8, NPTS), 0)
+    row = lax.broadcasted_iota(jnp.int32, (4, NPTS), 0)
 
     @pl.loop(0, NBLK, unroll=8)
     def _(b):
         o = own_ref[b]
         r = cnt_ref[o]
         cnt_ref[o] = r + 1
-        slot = o * 2 + jnp.minimum(r, 1)
+        r = jnp.minimum(r, 1)
+        slot_ref[b] = o * 2 + r
         at = pl.multiple_of(b * NPTS, NPTS)
-        v = jnp.broadcast_to(corner_ref[pl.ds(b, 1), :], (8, NPTS))
+        v = jnp.broadcast_to(corner_ref[pl.ds(b, 1), :], (4, NPTS))
         vx = div_const(v, 49)
         rest = v - vx * 49
         vy = div_const(rest, 7)
@@ -91,9 +103,13 @@
         head = jnp.where(
             row == 0, vx, jnp.where(row == 1, vy, jnp.where(row == 2, vz, cell_ref[b] + 1))
         )
-        tail = jnp.concatenate([w_ref[:, pl.ds(at, NPTS)].astype(F32), head.astype(F32)], 0)
-        send_ref[slot, 0:16, :] = feat_ref[:, pl.ds(at, NPTS)]
-        send_ref[slot, 16:32, :] = tail.astype(BF16)
+        send_ref[o, pl.ds(pl.multiple_of(r * 16, 16), 16), :] = feat_ref[:, pl.ds(at, NPTS)]
+        send_ref[o, pl.ds(pl.multiple_of(32 + r * 8, 8), 8), :] = w_ref[:, pl.ds(at, NPTS)]
+        head_ref[o, pl.ds(r * 4, 4), :] = head.astype(F32)
+
+    @pl.loop(0, NBLK // 8)
+    def _(i):
+        send_ref[pl.ds(i * 8, 8), 48:56, :] = head_ref[pl.ds(i * 8, 8)].astype(BF16)
 
 
 def pack(owner, cell, features, weights, corner):
@@ -101,18 +117,22 @@
     vmem = pl.BlockSpec(memory_space=pltpu.VMEM)
     return pl.pallas_call(
         pack_kernel,
-        out_shape=jax.ShapeDtypeStruct((NSLOT, 32, NPTS), BF16),
+        out_shape=(
+            jax.ShapeDtypeStruct((NBLK, 56, NPTS), BF16),
+            jax.ShapeDtypeStruct((NBLK,), jnp.int32),
+        ),
         in_specs=[smem, smem, vmem, vmem, vmem],
-        out_specs=vmem,
-        scratch_shapes=[pltpu.SMEM((NBLK,), jnp.int32)],
+        out_specs=(vmem, smem),
+        scratch_shapes=[pltpu.SMEM((NBLK,), jnp.int32), pltpu.VMEM((NBLK, 8, NPTS), F32)],
         name="pack",
     )(owner, cell, features, weights, corner)
 
 
-def yz_basis(tail):
+def yz_basis(w, head):
     zi = lax.broadcasted_iota(jnp.int32, (8, NPTS), 0).astype(F32)
-    bc = lambda k: jnp.broadcast_to(tail[k : k + 1, :], (8, NPTS))
-    vy, vz = bc(9), bc(10)
+    bc = lambda k: jnp.broadcast_to(w[k : k + 1, :], (8, NPTS))
+    vy = jnp.broadcast_to(head[1:2, :], (8, NPTS))
+    vz = jnp.broadcast_to(head[2:3, :], (8, NPTS))
     m0 = zi == vz
     m1 = zi == vz + 1.0
     zero = jnp.zeros((8, NPTS), F32)
@@ -149,7 +169,7 @@
     recv_hbm, tz_ref, field_hbm, out_hbm, ids_ref,
     recv_ref, g_ref, z_ref, field_ref, out_ref, in_sem, field_sem, out_sem, *, unroll
 ):
-    part = NSLOT // 4
+    part = NBLK // 4
 
     def fetch(k):
         at = pl.ds(k * part, part)
@@ -170,26 +190,32 @@
         @pl.loop(0, part // unroll)
         def _(i):
             for u in range(unroll):
-                s = k * part + i * unroll + u
-                tail = recv_ref[s, 16:32, :].astype(F32)
-                basis = yz_basis(tail)
-                feat = recv_ref[s, 0:16, :].astype(F32)
-                vx = jnp.broadcast_to(tail[8:9, :], (8, NPTS))
-                zf = jnp.zeros((8, NPTS), F32)
-                low, high = [], []
-                for ch in range(2):
-                    half = feat[ch * 8 : ch * 8 + 8]
-                    sel = [jnp.where(vx == float(x), half, 0.0) for x in range(7)]
-                    low += sel + [zf]
-                    high += [zf] + sel
-                lhs = jnp.concatenate(
-                    [jnp.concatenate(low, 0).astype(BF16), jnp.concatenate(high, 0).astype(BF16)],
-                    1,
-                )
-                res = mm(basis, lhs, NT)
-                b = jnp.clip(tail[11, 0].astype(jnp.int32) - 1, 0, 255)
-                ids_ref[s] = b
-                g_ref[b] = g_ref[b] + res
+                d = k * part + i * unroll + u
+                weights = recv_ref[d, 32:48, :].astype(F32)
+                heads = recv_ref[d, 48:56, :].astype(F32)
+                for j in range(2):
+                    head = heads[4 * j : 4 * j + 4]
+                    basis = yz_basis(weights[8 * j : 8 * j + 8], head)
+                    feat = recv_ref[d, 16 * j : 16 * j + 16, :].astype(F32)
+                    vx = jnp.broadcast_to(head[0:1, :], (8, NPTS))
+                    zf = jnp.zeros((8, NPTS), F32)
+                    low, high = [], []
+                    for ch in range(2):
+                        half = feat[ch * 8 : ch * 8 + 8]
+                        sel = [jnp.where(vx == float(x), half, 0.0) for x in range(7)]
+                        low += sel + [zf]
+                        high += [zf] + sel
+                    lhs = jnp.concatenate(
+                        [
+                            jnp.concatenate(low, 0).astype(BF16),
+                            jnp.concatenate(high, 0).astype(BF16),
+                        ],
+                        1,
+                    )
+                    res = mm(basis, lhs, NT)
+                    b = jnp.clip(head[3, 0].astype(jnp.int32) - 1, 0, 255)
+                    ids_ref[2 * d + j] = b
+                    g_ref[b] = g_ref[b] + res
 
     tz = tz_ref[...]
 
@@ -197,12 +223,10 @@
         at = pl.ds(q * 8, 8)
         return pltpu.make_async_copy(field_ref.at[at], field_hbm.at[at], field_sem.at[q])
 
-    def put_out(s, r):
-        return pltpu.make_async_copy(
-            out_ref.at[s, r], out_hbm.at[r * COLS + s], out_sem.at[s, r]
-        )
-
-    @pl.loop(0, 8)
+    def put_out(s):
+        return pltpu.make_async_copy(out_ref.at[s], out_hbm.at[:, s], out_sem.at[s])
+
+    @pl.loop(0, 8, unroll=2)
     def _(q):
         bx = q // 2
         by = q % 2
@@ -219,7 +243,7 @@
                 z_ref[bx, pl.ds(y, 128, stride=16), :] = res[:, e * 128 : e * 128 + 128]
         put_field(q).start()
 
-    @pl.loop(0, 16)
+    @pl.loop(0, 16, unroll=4)
     def _(s):
         for kz in range(4):
             for ri in range(2):
@@ -230,8 +254,7 @@
                     )
                     for ch in range(2):
                         out_ref[s, 2 * kz + ch, ri, p] = pair[ch].astype(BF16)
-        for r in range(8):
-            put_out(s, r).start()
+        put_out(s).start()
 
     @pl.loop(0, 8)
     def _(q):
@@ -239,8 +262,7 @@
 
     @pl.loop(0, 16)
     def _(s):
-        for r in range(8):
-            put_out(s, r).wait()
+        put_out(s).wait()
 
 
 def scatter(recv, tz):
@@ -251,20 +273,20 @@
         partial(scatter_kernel, unroll=16),
         out_shape=(
             jax.ShapeDtypeStruct((64, GRID, 128), BF16),
-            jax.ShapeDtypeStruct((128, 2, 2, 16, 128), BF16),
+            jax.ShapeDtypeStruct((8, 16, 2, 2, 16, 128), BF16),
             jax.ShapeDtypeStruct((NSLOT,), jnp.int32),
         ),
         in_specs=[hbm, vmem],
         out_specs=(hbm, hbm, smem),
         scratch_shapes=[
-            pltpu.VMEM((NSLOT, 32, NPTS), BF16),
+            pltpu.VMEM((NBLK, 56, NPTS), BF16),
             pltpu.VMEM((256, 64, 128), F32),
             pltpu.VMEM((4, 2048, 128), F32),
             pltpu.VMEM((64, GRID, 128), BF16),
             pltpu.VMEM((16, 8, 2, 2, 16, 128), BF16),
             pltpu.SemaphoreType.DMA((4,)),
             pltpu.SemaphoreType.DMA((8,)),
-            pltpu.SemaphoreType.DMA((16, 8)),
+            pltpu.SemaphoreType.DMA((16,)),
         ],
         name="scatter_z",
     )(recv, tz)
@@ -272,17 +294,17 @@
 
 def group_transpose(x):
     n = x.shape[0]
-    low, high = split_lanes(x[:, 0:8], x[:, 8:16])
-    x = jnp.concatenate([low, high], 0)
-    si = lax.broadcasted_iota(jnp.int32, x.shape, 1)
-    gi = lax.broadcasted_iota(jnp.int32, x.shape, 2) // 8
+    low, high = x[:, 0:8], x[:, 8:16]
+    even = (lax.broadcasted_iota(jnp.int32, low.shape, 2) // 8) % 2 == 0
+    first = jnp.where(even, low, pltpu.roll(high, 8, 2))
+    second = jnp.where(even, pltpu.roll(low, 120, 2), high)
+    x = jnp.concatenate([first, second], 0)
+    group = lax.broadcasted_iota(jnp.int32, x.shape, 2) // 16
+    x = pltpu.roll(x, 0, 2, stride=16, stride_axis=1)
     for k in range(3):
         d = 1 << k
-        mi = (si // d) % 2
-        mg = (gi // d) % 2
-        up = pltpu.roll(pltpu.roll(x, 8 - d, 1), 8 * d, 2)
-        down = pltpu.roll(pltpu.roll(x, d, 1), 128 - 8 * d, 2)
-        x = jnp.where(mi == mg, x, jnp.where(mi < mg, up, down))
+        x = jnp.where((group // d) % 2 == 1, pltpu.roll(x, 8 - d, 1), x)
+    x = pltpu.roll(x, 0, 2, stride=16, stride_axis=1)
     return jnp.concatenate([x[:n], x[n:]], 1)
 
 
@@ -294,7 +316,7 @@
     for r in range(8):
         get(r).start()
 
-    @pl.loop(0, 8)
+    @pl.loop(0, 8, unroll=2)
     def _(r):
         get(r).wait()
         at = pl.ds(r * COLS, COLS)
@@ -369,13 +391,13 @@
         at = pl.ds(r * COLS, COLS)
         return pltpu.make_async_copy(out_ref.at[at], out_hbm.at[at], sem.at[r])
 
-    @pl.loop(0, 4)
+    @pl.loop(0, 4, unroll=2)
     def _(g):
         rhs = in_ref[pl.ds(2 * g, 2)].reshape(128, 128)
         xi = group_transpose(mm(ix_ref[...], rhs, NT).reshape(32, 16, 128))
         u_ref[g] = xi.astype(BF16)
 
-    @pl.loop(0, 8)
+    @pl.loop(0, 8, unroll=2)
     def _(r):
         rhs = jnp.concatenate(
             [u_ref[:, pl.ds(r * 4 + p * 2, 2)].reshape(128, 128) for p in range(2)], 1
@@ -417,41 +439,56 @@
     return h + h * t
 
 
+def expand_weights(in_ref, skip_ref, out_ref, w1_ref, w2_ref):
+    iota = lambda shape, d: lax.broadcasted_iota(jnp.int32, shape, d)
+    hot = lambda cond: jnp.where(cond, 1.0, 0.0).astype(BF16)
+    rep = hot(iota((HID, 512), 0) == iota((HID, 512), 1) % HID)
+    row = iota((128, CH), 0)
+    chan = hot((row // 64) * 8 + row % 8 == iota((128, CH), 1))
+    keep = (iota((128, 512), 0) // 8) % 8 == iota((128, 512), 1) // HID
+    first = in_ref[...]
+    both = mm(skip_ref[...], first, TN).astype(BF16)
+    for e, w in enumerate((first, both)):
+        full = mm(chan, mm(w, rep).astype(BF16))
+        w1_ref[e * 128 : e * 128 + 128, :] = jnp.where(keep, full, 0.0).astype(BF16)
+    rows = hot(iota((512, HID), 0) % HID == iota((512, HID), 1))
+    cols = hot(iota((CH, 128), 1) % CH == iota((CH, 128), 0))
+    full = mm(mm(rows, out_ref[...], NT).astype(BF16), cols)
+    keep = iota((512, 128), 0) // HID == iota((512, 128), 1) // CH
+    w2_ref[...] = jnp.where(keep, full, 0.0).astype(BF16)
+
+
 def final_kernel(
-    ids_ref, yi_hbm, field_hbm, recv_hbm, iz_ref, w1_ref, b1_ref, w2_ref, out_hbm,
-    yi_ref, field_ref, tail_ref, out_ref, y_ref, x_ref, l_ref,
+    ids_ref, yi_hbm, field_hbm, recv_hbm, iz_ref, in_ref, skip_ref, bias_ref, mout_ref, out_hbm,
+    yi_ref, field_ref, tail_ref, out_ref, y_ref, xa_ref, xb_ref, l_ref, w1_ref, w2_ref, b1_ref,
     yi_sem, field_sem, tail_sem, out_sem, *, ny, unroll
 ):
     def get_yi(r):
         at = pl.ds(r * COLS, COLS)
         return pltpu.make_async_copy(yi_hbm.at[at], yi_ref.at[at], yi_sem.at[r])
 
-    def get_field(i):
-        at = pl.ds(i * ny, ny)
-        return pltpu.make_async_copy(field_hbm.at[at], field_ref.at[at], field_sem.at[i])
-
     def put_out(i):
-        at = pl.ds(i * unroll, unroll)
+        at = pl.ds(i * 2 * unroll, 2 * unroll)
         return pltpu.make_async_copy(out_ref.at[at], out_hbm.at[at], out_sem.at[i])
 
-    get_tail = pltpu.make_async_copy(recv_hbm.at[:, 16:32], tail_ref, tail_sem)
+    get_field = pltpu.make_async_copy(field_hbm, field_ref, field_sem)
+    get_tail = pltpu.make_async_copy(recv_hbm.at[:, 32:56], tail_ref, tail_sem)
 
     @pl.loop(0, 8)
     def _(r):
         get_yi(r).start()
 
-    @pl.loop(0, 64 // ny)
-    def _(i):
-        get_field(i).start()
-
+    get_field.start()
     get_tail.start()
+    expand_weights(in_ref, skip_ref, mout_ref, w1_ref, w2_ref)
+    b1_ref[...] = jnp.concatenate([bias_ref[...]] * 8, 1)
 
     @pl.loop(0, 4)
     def _(kz):
         get_yi(2 * kz).wait()
         get_yi(2 * kz + 1).wait()
 
-        @pl.loop(0, 16)
+        @pl.loop(0, 16, unroll=4)
         def _(s):
             for ri in range(2):
                 at = pl.multiple_of(s * 128 + kz * 32 + ri * 16, 16)
@@ -463,11 +500,9 @@
                     for e in range(2):
                         y_ref[2 * p + e, pl.ds(at, 16), :] = pair[e]
 
-    @pl.loop(0, 64 // ny)
-    def _(i):
+    def stage(i, x_ref):
         base = i * ny
         bx = base // 16
-        get_field(i).wait()
         for p in range(ny // 2):
             y = (base + 2 * p) % 16
             rhs = jnp.concatenate(
@@ -478,79 +513,94 @@
                 at = (2 * p + e) * GRID
                 x_ref[at : at + GRID, 0:128] = res[:, e * 128 : e * 128 + 128]
                 x_ref[at : at + GRID, 128:256] = field_ref[base + 2 * p + e]
+
+    def layer(i, x_ref):
         h = gelu(mm(x_ref[...], w1_ref[...]) + b1_ref[...])
         o = mm(h, w2_ref[...]).astype(BF16).astype(F32)
-        l_ref[pl.ds(base, ny)] = o.reshape(ny, GRID, 128)
+        l_ref[pl.ds(i * ny, ny)] = o.reshape(ny, GRID, 128)
+
+    steps = 64 // ny
+    get_field.wait()
+    stage(0, xa_ref)
+
+    @pl.loop(0, steps // 2)
+    def _(i):
+        stage(2 * i + 1, xb_ref)
+        layer(2 * i, xa_ref)
+        stage(jnp.minimum(2 * i + 2, steps - 1), xa_ref)
+        layer(2 * i + 1, xb_ref)
 
     get_tail.wait()
 
-    @pl.loop(0, NSLOT // unroll)
+    @pl.loop(0, NBLK // unroll)
     def _(i):
         for u in range(unroll):
-            s = i * unroll + u
-            tail = tail_ref[s].astype(F32)
-            basis = yz_basis(tail)
-            b = ids_ref[s]
-            q = b // 32
-            at = pl.multiple_of((b % 32) * 8, 8)
-            cells = l_ref[pl.ds(q * 8, 8), pl.ds(at, 8), :].reshape(64, 128).astype(BF16)
-            res = mm(cells, basis, TN)
-            vx = jnp.broadcast_to(tail[8:9, :], (16, NPTS))
-            val = jnp.zeros((16, NPTS), F32)
-            for x in range(7):
-                got = res[x * 16 : x * 16 + 16, 0:128] + res[x * 16 + 16 : x * 16 + 32, 128:256]
-                val = jnp.where(vx == float(x), got, val)
-            out_ref[s] = val.astype(BF16)
+            d = i * unroll + u
+            weights = tail_ref[d, 0:16, :].astype(F32)
+            heads = tail_ref[d, 16:24, :].astype(F32)
+            for j in range(2):
+                head = heads[4 * j : 4 * j + 4]
+                basis = yz_basis(weights[8 * j : 8 * j + 8], head)
+                b = ids_ref[2 * d + j]
+                q = b // 32
+                at = pl.multiple_of((b % 32) * 8, 8)
+                cells = l_ref[pl.ds(q * 8, 8), pl.ds(at, 8), :].reshape(64, 128).astype(BF16)
+                res = mm(cells, basis, TN)
+                vx = jnp.broadcast_to(head[0:1, :], (16, NPTS))
+                val = jnp.zeros((16, NPTS), F32)
+                for x in range(7):
+                    got = (
+                        res[x * 16 : x * 16 + 16, 0:128]
+                        + res[x * 16 + 16 : x * 16 + 32, 128:256]
+                    )
+                    val = jnp.where(vx == float(x), got, val)
+                out_ref[2 * d + j] = val.astype(BF16)
         put_out(i).start()
 
-    @pl.loop(0, NSLOT // unroll)
+    @pl.loop(0, NBLK // unroll)
     def _(i):
         put_out(i).wait()
 
 
-def final(ids, yi, field, recv, iz, w1, b1, w2):
+def final(ids, yi, field, recv, iz, first, skip, bias, mout):
     smem = pl.BlockSpec(memory_space=pltpu.SMEM)
     vmem = pl.BlockSpec(memory_space=pltpu.VMEM)
     hbm = pl.BlockSpec(memory_space=pl.ANY)
-    ny, unroll = 8, 32
+    ny, unroll = 8, 16
     return pl.pallas_call(
         partial(final_kernel, ny=ny, unroll=unroll),
         out_shape=jax.ShapeDtypeStruct((NSLOT, 16, NPTS), BF16),
-        in_specs=[smem, hbm, hbm, hbm, vmem, vmem, vmem, vmem],
+        in_specs=[smem, hbm, hbm, hbm, vmem, vmem, vmem, vmem, vmem],
         out_specs=hbm,
         scratch_shapes=[
             pltpu.VMEM((128, 2, 2, 16, 128), BF16),
             pltpu.VMEM((64, GRID, 128), BF16),
-            pltpu.VMEM((NSLOT, 16, NPTS), BF16),
+            pltpu.VMEM((NBLK, 24, NPTS), BF16),
             pltpu.VMEM((NSLOT, 16, NPTS), BF16),
             pltpu.VMEM((4, 2048, 128), F32),
             pltpu.VMEM((ny * GRID, 256), BF16),
+            pltpu.VMEM((ny * GRID, 256), BF16),
             pltpu.VMEM((64, GRID, 128), F32),
+            pltpu.VMEM((256, 512), BF16),
+            pltpu.VMEM((512, 128), BF16),
+            pltpu.VMEM((1, 512), F32),
             pltpu.SemaphoreType.DMA((8,)),
-            pltpu.SemaphoreType.DMA((64 // ny,)),
             pltpu.SemaphoreType.DMA,
-            pltpu.SemaphoreType.DMA((NSLOT // unroll,)),
+            pltpu.SemaphoreType.DMA,
+            pltpu.SemaphoreType.DMA((NBLK // unroll,)),
         ],
         name="mlp_gather",
-    )(ids, yi, field, recv, iz, w1, b1, w2)
-
-
-def unpack_kernel(own_ref, in_ref, out_ref, cnt_ref):
-    @pl.loop(0, NBLK, unroll=16)
-    def _(i):
-        cnt_ref[i] = 0
-
+    )(ids, yi, field, recv, iz, first, skip, bias, mout)
+
+
+def unpack_kernel(slot_ref, in_ref, out_ref):
     @pl.loop(0, NBLK, unroll=8)
     def _(b):
-        o = own_ref[b]
-        r = cnt_ref[o]
-        cnt_ref[o] = r + 1
-        slot = o * 2 + jnp.minimum(r, 1)
         at = pl.multiple_of(b * NPTS, NPTS)
-        out_ref[:, pl.ds(at, NPTS)] = in_ref[slot]
-
-
-def unpack(owner, vals):
+        out_ref[:, pl.ds(at, NPTS)] = in_ref[slot_ref[b]]
+
+
+def unpack(slots, vals):
     smem = pl.BlockSpec(memory_space=pltpu.SMEM)
     vmem = pl.BlockSpec(memory_space=pltpu.VMEM)
     return pl.pallas_call(
@@ -558,9 +608,8 @@
         out_shape=jax.ShapeDtypeStruct((CH, NBLK * NPTS), BF16),
         in_specs=[smem, vmem],
         out_specs=vmem,
-        scratch_shapes=[pltpu.SMEM((NBLK,), jnp.int32)],
         name="unpack",
-    )(owner, vals)
+    )(slots, vals)
 
 
 def a2a(x, axes):
@@ -580,23 +629,20 @@
     mlp_out,
 ):
     tz, ty, tx, ix, iy, iz = tables()
-    eye = jnp.eye(8, dtype=BF16)
-    both = jnp.dot(mlp_in, skip_weight, preferred_element_type=F32).astype(BF16)
-    w1 = jnp.stack([jnp.kron(eye, mlp_in.T), jnp.kron(eye, both.T)], 0)
-    w1 = w1.reshape(2, 8, 2, 8, 512).transpose(0, 2, 1, 3, 4).reshape(256, 512)
-    w2 = jnp.kron(eye, mlp_out.T)
-    b1 = jnp.tile(mlp_bias, 8)[None, :]
     owner = block_owner.reshape(NBLK)
-    send = pack(owner, block_cell, features, point_weights, point_corner.reshape(NBLK, NPTS))
+    send, slots = pack(
+        owner, block_cell, features, point_weights, point_corner.reshape(NBLK, NPTS)
+    )
     recv = a2a(send, ("row", "col"))
     field, zs, ids = scatter(recv, tz)
-    zs = a2a(zs, ("row", "col"))
+    zs = a2a(zs.reshape(128, 2, 2, 16, 128), ("row", "col"))
     spec = a2a(yx_forward(zs, ty, tx), "row")
     mixed = a2a(mix(spec, spec_weight), "row")
     yi = a2a(xy_inverse(mixed, ix, iy), ("row", "col"))
-    vals = final(ids, yi, field, recv, iz, w1, b1, w2)
-    vals = a2a(vals, ("row", "col"))
-    return unpack(owner, vals)
+    vals = final(
+        ids, yi, field, recv, iz, mlp_in.T, skip_weight, mlp_bias.reshape(1, HID), mlp_out
+    )
+    return unpack(slots, a2a(vals, ("row", "col")))
 
 
 def solution(mesh):

time: 226 us -> 213 us (0.942)
  blocking collectives: 122 us -> 155 us
  waiting for transfers between devices: 26.2 us -> 0 us
  Pallas kernels: 67.1 us -> 57.8 us
  starting transfers between devices: 4.47 us -> 0 us
  local copies, waits for them, and re-layouts: 3.5 us -> 0 us
    all_to_all x5 -> x6, blocking collectives: 122 us -> 155 us  [a2a(): return lax.all_to_all(x, axes, split_axis=0, concat_axis=0, tiled=True)]
    all_to_all x1 -> x0, waiting for transfers between devices: 26.2 us -> none  [a2a(): return lax.all_to_all(x, axes, split_axis=0, concat_axis=0, tiled=True)]
    all_to_all x1 -> x0, starting transfers between devices: 4.47 us -> none  [a2a(): return lax.all_to_all(x, axes, split_axis=0, concat_axis=0, tiled=True)]
    pallas_call x1, Pallas kernels: 27.2 us -> 23.2 us  [final(): pl.pallas_call(partial(final_kernel, ny=ny, unroll=unroll), out_shape=jax...]
    pallas_call x1, Pallas kernels: 16.6 us -> 13.2 us  [scatter(): pl.pallas_call(partial(scatter_kernel, unroll=16), out_shape=(jax.ShapeDt...]
  transfers between devices with their start and end apart: 1 -> 0, of which waited for: 1 -> 0; matrix products, arithmetic and copies ran while one was open for 1% -> 0% of each run, Pallas kernels for 0% -> 0%
where the time goes in v3:
time: 213 us
  blocking collectives  155 us (73%)
  Pallas kernels  57.8 us (27%)
    all_to_all x6, blocking collectives, a2a(): return lax.all_to_all(x, axes, split_axis=0, concat_axis=0, tiled=True)  155 us
    pallas_call x1, Pallas kernels, final(): pl.pallas_call(partial(final_kernel, ny=ny, unroll=unroll), out_shape=jax...  23.2 us
    pallas_call x1, Pallas kernels, scatter(): pl.pallas_call(partial(scatter_kernel, unroll=16), out_shape=(jax.ShapeDt...  13.2 us
    pallas_call x1, Pallas kernels, yx_forward(): pl.pallas_call(yx_kernel, out_shape=jax.ShapeDtypeStruct((8, 64, 128), BF...  6.51 us
    pallas_call x1, Pallas kernels, pack(): pl.pallas_call(pack_kernel, out_shape=(jax.ShapeDtypeStruct((NBLK, 56, NP...  4.32 us

profile of v3, /device:TPU:1, one launch (start us, length us, event | category | flops | bytes accessed | tf_op | source)
XLA Modules:
  0.0 212.6 jit_solution(16854929804845833805)
XLA Ops:
  0.0 4.3 %pack.1 = (bf16[128,56,128]{2,1,0:T(8,128)(2,1)}, s32[128]{0:T(128)}) custom-call(s32[128]{0:T(128)} %bitcast.8, s32[128]{0:T(128)} %cell_ref.1, bf16[16,16384]{1,0:T(8,128)(2,1)} %feat_ref.1, bf16[8,16384]{1,0:T(8,128)(2,1)} %w_ref.2, s32[128,128]{1,0:T(8,128)} %bitcast.6), custom_call_target="tpu_custom_call" | custom-call | tf_op jit(solution)/shard_map/pack/pallas_call | solution.py:118
  4.3 38.4 %all_to_all.30.recv_hbm = bf16[128,56,128]{2,1,0:T(8,128)(2,1)} all-to-all(bf16[128,56,128]{2,1,0:T(8,128)(2,1)} %get-tuple-element.11), channel_id=1, replica_groups=mesh['row'=8,'col'=16] {'row','col'}, dimensions={0} | all-to-all | bytes 3670016 | tf_op jit(solution)/shard_map/all_to_all | solution.py:616
  42.7 13.2 %scatter_z.1 = (bf16[64,256,128]{2,1,0:T(8,128)(2,1)}, bf16[8,16,2,2,16,128]{5,4,3,2,1,0:T(8,128)(2,1)}, s32[256]{0:T(256)}) custom-call(bf16[128,56,128]{2,1,0:T(8,128)(2,1)} %all_to_all.30.recv_hbm, bf16[128,256]{1,0:T(8,128)(2,1)} %constant.19.tz_ref), custom_call_target="tpu_custom_call" | custom-call | tf_op jit(solution)/shard_map/scatter_z/pallas_call | solution.py:272
  55.9 35.4 %all_to_all.31.in_hbm = bf16[128,2,2,16,128]{4,3,2,1,0:T(8,128)(2,1)} all-to-all(bf16[128,2,2,16,128]{4,3,2,1,0:T(8,128)(2,1)} %bitcast.5), channel_id=1, replica_groups=mesh['row'=8,'col'=16] {'row','col'}, dimensions={0} | all-to-all | bytes 4194304 | tf_op jit(solution)/shard_map/all_to_all | solution.py:616
  91.4 6.5 %yx_forward.1 = bf16[8,64,128]{2,1,0:T(8,128)(2,1)} custom-call(bf16[128,2,2,16,128]{4,3,2,1,0:T(8,128)(2,1)} %all_to_all.31.in_hbm, bf16[128,512]{1,0:T(8,128)(2,1)} %constant.20.ty_ref, bf16[128,512]{1,0:T(8,128)(2,1)} %constant.21.tx_ref), custom_call_target="tpu_custom_call" | custom-call | tf_op jit(solution)/shard_map/yx_forward/pallas_call | solution.py:341
  97.9 10.7 %all_to_all.32.in_ref = bf16[8,64,128]{2,1,0:T(8,128)(2,1)} all-to-all(bf16[8,64,128]{2,1,0:T(8,128)(2,1)} %yx_forward.1), channel_id=1, replica_groups=mesh['row'=8,'col'=16] {'row'}, dimensions={0} | all-to-all | bytes 262144 | tf_op jit(solution)/shard_map/all_to_all | solution.py:616
  108.5 4.1 %mix.1 = bf16[8,64,128]{2,1,0:T(8,128)(2,1)} custom-call(bf16[8,64,128]{2,1,0:T(8,128)(2,1)} %all_to_all.32.in_ref, bf16[4,8,16,16,128]{4,3,2,1,0:T(8,128)(2,1)} %w_ref.3), custom_call_target="tpu_custom_call" | custom-call | tf_op jit(solution)/shard_map/mix/pallas_call | solution.py:376
  112.6 10.1 %all_to_all.33.in_ref = bf16[8,64,128]{2,1,0:T(8,128)(2,1)} all-to-all(bf16[8,64,128]{2,1,0:T(8,128)(2,1)} %mix.1), channel_id=1, replica_groups=mesh['row'=8,'col'=16] {'row'}, dimensions={0} | all-to-all | bytes 262144 | tf_op jit(solution)/shard_map/all_to_all | solution.py:616
  122.7 4.1 %xy_inverse.1 = bf16[128,2,2,16,128]{4,3,2,1,0:T(8,128)(2,1)} custom-call(bf16[8,64,128]{2,1,0:T(8,128)(2,1)} %all_to_all.33.in_ref, bf16[512,128]{1,0:T(8,128)(2,1)} %constant.22.ix_ref, bf16[512,128]{1,0:T(8,128)(2,1)} %constant.23.iy_ref), custom_call_target="tpu_custom_call" | custom-call | tf_op jit(solution)/shard_map/xy_inverse/pallas_call | solution.py:420
  126.8 34.8 %all_to_all.34.yi_hbm = bf16[128,2,2,16,128]{4,3,2,1,0:T(8,128)(2,1)} all-to-all(bf16[128,2,2,16,128]{4,3,2,1,0:T(8,128)(2,1)} %xy_inverse.1), channel_id=1, replica_groups=mesh['row'=8,'col'=16] {'row','col'}, dimensions={0} | all-to-all | bytes 4194304 | tf_op jit(solution)/shard_map/all_to_all | solution.py:616
  161.6 23.2 %mlp_gather.1 = bf16[256,16,128]{2,1,0:T(8,128)(2,1)} custom-call(s32[256]{0:T(256)} %get-tuple-element.12.ids_ref, bf16[128,2,2,16,128]{4,3,2,1,0:T(8,128)(2,1)} %all_to_all.34.yi_hbm, bf16[64,256,128]{2,1,0:T(8,128)(2,1)} %get-tuple-element.14.field_hbm, bf16[128,56,128]{2,1,0:T(8,128)(2,1)} %all_to_all.30.recv_hbm, bf16[256,128]{1,0:T(8,128)(2,1)} %constant.24.iz_ref, ...), custom_call_target="tpu_custom_call" | custom-call | tf_op jit(solution)/shard_map/mlp_gather/pallas_call | solution.py:570
  184.9 25.3 %all_to_all.35.in_ref = bf16[256,16,128]{2,1,0:T(8,128)(2,1)} all-to-all(bf16[256,16,128]{2,1,0:T(8,128)(2,1)} %mlp_gather.1), channel_id=1, replica_groups=mesh['row'=8,'col'=16] {'row','col'}, dimensions={0} | all-to-all | bytes 2097152 | tf_op jit(solution)/shard_map/all_to_all | solution.py:616
  210.2 2.4 %unpack.1 = bf16[16,16384]{1,0:T(8,128)(2,1)} custom-call(s32[128]{0:T(128)} %get-tuple-element.10.slot_ref, bf16[256,16,128]{2,1,0:T(8,128)(2,1)} %all_to_all.35.in_ref), custom_call_target="tpu_custom_call" | custom-call | tf_op jit(solution)/shard_map/unpack/pallas_call | solution.py:606
